TPU v7x, 32 devices: a whole 2x2x4 slice. The times are simulated.
32 devices in a mesh: group: 2 (over y), seq: 4 (over z), mp: 4 (over x, core).
Axes of the slice: x: 2, y: 2, z: 4, core: 2. Of those that a mesh axis runs over, the one named last changes fastest.
Arguments:
- embeds: bfloat16 [8192, 8192], P('seq', 'mp'), may hold values from -250 to 250
- image_feats: bfloat16 [512, 7296], P('seq'), may hold values from -6 to 6
- image_pos: int32 [512], P('seq'), may hold values from 0 to 8191, as said below
- proj_w: bfloat16 [7296, 8192], P('seq', 'mp'), may hold values from -0.0625 to 0.0625
- proj_b: bfloat16 [8192], P('mp'), may hold values from -3 to 3
- norm_gain: bfloat16 [8192], P('mp'), may hold values from 0.099609375 to 1.8984375
- kv_w: bfloat16 [8192, 2048], P('mp'), may hold values from -0.0625 to 0.0625
- prompt_lengths: int32 [2], replicated, may hold values from 2048 to 4096
- page_owner: int32 [512, 1], P('seq'), may hold values from 0 to 3; in each aligned block of 128 rows (0 to 127, 128 to 255, ...) at most 64 rows name the same one
- queries: bfloat16 [512, 8192], P('seq', 'mp'), may hold values from -180 to 180
- kv_cache: bfloat16 [512, 128, 2048], P('seq', None, 'mp'), may hold values from -5 to 5
- new_kv: bfloat16 [512, 2048], P('seq', 'mp'), may hold values from -5 to 5
- cache_lengths: int32 [512], P('seq'), may hold values from 2 to 128
Outputs:
- page_slots: bfloat16 [2048, 16, 2048], P(('group', 'seq'), None, 'mp')
- row_states: bfloat16 [1024, 8192], P(('group', 'seq'), 'mp')
Inputs may be any that keep to these rules, and one draw needn't show every extreme that they name: `image_pos`: distinct and increasing; entries s * 128 to (s + 1) * 128 - 1 lie among tokens s * 2048 to (s + 1) * 2048 - 1. `page_owner`: among the 128 pages of one seq index no owner is named more than 64 times.
All inputs are finite; a program needn't handle non-finite values.
Results may differ from a plain program's by a relative error of at most 0.005.
Values may be sent and summed in bfloat16 or wider, within the bound.
A program may use at most 128 MiB of HBM per device.

v0:
```python
import functools

import jax
import jax.numpy as jnp
from jax import lax
from jax.experimental import pallas as pl
from jax.experimental.pallas import tpu as pltpu
from jax.sharding import PartitionSpec as P

HEAD = 128
LANES = 128
TILE = 512
CORES = 2
MESH = pl.DeviceIdType.MESH
F32 = jnp.float32
BF16 = jnp.bfloat16


def gated(condition, action, empty_value, *operands):
    return lax.cond(condition, action, lambda *unused: empty_value, *operands)


def attend_head(queries, keys, values, fresh_key, fresh_value, in_cache):
    scores = jnp.einsum(
        "rqh,rjh->rqj", queries, keys, preferred_element_type=jnp.float32
    ) * HEAD ** (-0.5)
    scores = jnp.where(in_cache[:, None, :], scores, -1e30)
    own_score = jnp.einsum(
        "rqh,rh->rq", queries, fresh_key, preferred_element_type=jnp.float32
    ) * HEAD ** (-0.5)
    row_max = jnp.maximum(jnp.max(scores, axis=2), own_score)
    weights = jnp.exp(scores - row_max[..., None])
    own_weight = jnp.exp(own_score - row_max)
    denominator = jnp.sum(weights, axis=2) + own_weight
    probability = (weights / denominator[..., None]).astype(jnp.bfloat16)
    own_prob = lax.optimization_barrier((own_weight / denominator).astype(jnp.bfloat16)).astype(
        jnp.float32
    )
    attended = jnp.einsum("rqj,rjh->rqh", probability, values, preferred_element_type=jnp.float32)
    attended = attended + own_prob[..., None] * fresh_value[:, None, :].astype(jnp.float32)
    return attended.astype(jnp.bfloat16)


def attend(queries, kv_cache, new_kv, cache_lengths):
    row_count = queries.shape[0]
    heads_kv = kv_cache.shape[2] // (2 * HEAD)
    share = queries.shape[1] // heads_kv
    in_cache = jnp.arange(kv_cache.shape[1], dtype=jnp.int32)[None, :] < cache_lengths[:, None]
    heads = []
    for head in range(heads_kv):
        key, value, end = 2 * HEAD * head, 2 * HEAD * head + HEAD, 2 * HEAD * (head + 1)
        attended = attend_head(
            queries[:, head * share : (head + 1) * share].reshape(row_count, share // HEAD, HEAD),
            kv_cache[:, :, key:value],
            kv_cache[:, :, value:end],
            new_kv[:, key:value],
            new_kv[:, value:end],
            in_cache,
        )
        heads.append(attended.reshape(row_count, share))
    return jnp.concatenate(heads, axis=1)


def live_rows(positions, prompt_lengths, prompt_len):
    prompt_ids = positions // prompt_len
    match = prompt_ids[..., None] == jnp.arange(prompt_lengths.shape[0], dtype=jnp.int32)
    limit = jnp.sum(jnp.where(match, prompt_lengths, 0), axis=-1)
    return positions % prompt_len < limit


def ds(index, size):
    return pl.ds(pl.multiple_of(index * size, size), size)


def spread_rows(row):
    return jnp.transpose(jnp.broadcast_to(row, (LANES, LANES)))


def prefill_kernel(
    groups,
    seqs,
    mps,
    page,
    width,
    embeds,
    feats,
    proj_w,
    bias,
    gain,
    kv_w,
    sel,
    mask,
    dest,
    slots_out,
    hid_out,
    img_out,
    dest_out,
    e_buf,
    w_buf,
    pw_buf,
    f_buf,
    acc1,
    s1,
    r1,
    acc2,
    s2,
    r2,
    sq_own,
    sq_recv,
    scale,
    outf,
    by_owner,
    arrived,
    p_own,
    p_send,
    p_recv,
    hid,
    i_scaled,
    i_acc,
    is1,
    ir1,
    is2,
    ir2,
    isq_own,
    isq_recv,
    ikv,
    load_sem,
    w_sem,
    e_sem,
    pw_sem,
    fl_sem,
    send1,
    recv1,
    send2,
    recv2,
    send_sq,
    recv_sq,
    send_f,
    recv_f,
    send_fc,
    recv_fc,
    send_r,
    recv_r,
    send_h,
    recv_h,
    send_i1,
    recv_i1,
    send_i2,
    recv_i2,
    send_iq,
    recv_iq,
    send_z,
    recv_z,
    send_y,
    recv_y,
    loc_sem,
    send_iz,
    recv_iz,
    send_iy,
    recv_iy,
    send_if,
    recv_if,
    send_d,
    recv_d,
    misc_sem,
):
    g = lax.axis_index("group")
    s = lax.axis_index("seq")
    m = lax.axis_index("mp")
    chips = mps // CORES
    chip = m // CORES
    core = m % CORES
    partner = chip * CORES + (1 - core)
    peer = 1 - g
    chunks, feat_local, _ = w_buf.shape
    tokens = e_buf.shape[0]
    tiles = tokens // TILE
    steps = chunks * tiles
    rows_img = hid.shape[0]
    half_rows = rows_img // groups
    core_rows = half_rows // CORES
    cols = chunks * LANES
    block_cols = cols * groups
    slots = sel.shape[0]
    pages = sel.shape[1]
    block = slots * page // seqs
    own_cols = chips * LANES

    def remote(src, dst, send, recv, **where):
        return pltpu.make_async_remote_copy(
            src_ref=src,
            dst_ref=dst,
            send_sem=send,
            recv_sem=recv,
            device_id=where,
            device_id_type=MESH,
        )

    def seq_at(k):
        return lax.rem(s + k, seqs)

    def seq_from(k):
        return lax.rem(s + seqs - k, seqs)

    def mp_at(k):
        return lax.rem(m + k, mps)

    def chip_at(k):
        return lax.rem(chip + k, chips) * CORES + core

    def e_copy(i):
        return pltpu.make_async_copy(embeds.at[ds(i, TILE), :], e_buf.at[ds(i, TILE), :], e_sem.at[i])

    def w_copy(c, q, k):
        target = lax.rem(chip + k, chips) * CORES + (core if q == 0 else 1 - core)
        start = target * block_cols + g * cols + c * LANES
        return pltpu.make_async_copy(
            kv_w.at[:, pl.ds(pl.multiple_of(start, LANES), LANES)],
            w_buf.at[c, :, (q * chips + k) * LANES : (q * chips + k + 1) * LANES],
            w_sem.at[c, q * chips + k],
        )

    e_copy(0).start()
    for q in range(CORES):
        for k in range(chips):
            w_copy(0, q, k).start()
    for i in range(1, tiles):
        e_copy(i).start()
    for c in range(1, chunks):
        for q in range(CORES):
            for k in range(chips):
                w_copy(c, q, k).start()
    pw_copy = pltpu.make_async_copy(proj_w, pw_buf, pw_sem)
    pw_copy.start()
    own_feats = pltpu.make_async_copy(feats.at[s], f_buf.at[s], fl_sem)
    own_feats.start()

    barrier = pltpu.get_barrier_semaphore()
    for k in range(1, seqs):
        pl.semaphore_signal(barrier, inc=1, device_id={"seq": seq_at(k)}, device_id_type=MESH)
    for k in range(1, mps):
        pl.semaphore_signal(barrier, inc=1, device_id={"mp": mp_at(k)}, device_id_type=MESH)
    pl.semaphore_signal(barrier, inc=1, device_id={"group": peer}, device_id_type=MESH)
    pl.semaphore_wait(barrier, seqs - 1 + mps - 1 + 1)

    def f_send(k):
        rows = ds(core, core_rows)
        return remote(
            feats.at[seq_at(k), rows, :],
            f_buf.at[s, rows, :],
            send_f.at[k - 1],
            recv_f.at[k - 1],
            seq=seq_at(k),
        )

    def f_share(k):
        rows = ds(core, core_rows)
        src = seq_from(k)
        return remote(
            f_buf.at[src, rows, :],
            f_buf.at[src, rows, :],
            send_fc.at[k - 1],
            recv_fc.at[k - 1],
            mp=partner,
        )

    def d_send(k):
        return remote(dest, dest_out.at[s], send_d.at[k - 1], recv_d.at[k - 1], seq=seq_at(k))

    for k in range(1, seqs):
        f_send(k).start()
    for k in range(1, seqs):
        d_send(k).start()
    d_local = pltpu.make_async_copy(dest, dest_out.at[s], misc_sem.at[0])
    d_local.start()

    def first(n):
        return remote(s1.at[n], r1.at[n], send1.at[n], recv1.at[n], mp=partner)

    def second(n, k):
        return remote(
            s2.at[n, k - 1], r2.at[n, k - 1], send2.at[n, k - 1], recv2.at[n, k - 1], mp=chip_at(k)
        )

    def sq_send(k):
        return remote(sq_own, sq_recv.at[k - 1], send_sq.at[k - 1], recv_sq.at[k - 1], mp=mp_at(k))

    def p_copy(k):
        return remote(
            p_send.at[seq_at(k)], p_recv.at[k - 1], send_r.at[k - 1], recv_r.at[k - 1], seq=seq_at(k)
        )

    def scale_tile(i):
        e_copy(i).wait()

        def body(b, carry):
            rows = ds(i * (TILE // LANES) + b, LANES)
            total = jnp.zeros((LANES, LANES), F32)
            for j in range(feat_local // LANES):
                at = slice(j * LANES, (j + 1) * LANES)
                value = e_buf[rows, at].astype(F32)
                total = total + value * value
                e_buf[rows, at] = (value * gain[:, at].astype(F32)).astype(BF16)
            sq_own[pl.ds(i * (TILE // LANES) + b, 1), :] = jnp.sum(
                jnp.transpose(total), axis=0, keepdims=True
            )
            return carry

        lax.fori_loop(0, TILE // LANES, body, 0)

    col_tile = min(512, feat_local)

    def project():
        for k in range(1, seqs):
            f_share(k).wait()
        own_feats.wait()
        pw_copy.wait()
        spread = f_buf[...].reshape(seqs * half_rows, f_buf.shape[2])

        def body(t, carry):
            at = ds(t, col_tile)
            out = jnp.dot(spread, pw_buf[:, at], preferred_element_type=F32)
            out = out.reshape(seqs, half_rows, col_tile)
            p_send[:, :, at] = out.astype(BF16)
            p_own[:, :, at] = out
            for k in range(1, seqs):
                remote(
                    p_send.at[seq_at(k), :, at],
                    p_recv.at[k - 1, :, at],
                    send_r.at[k - 1],
                    recv_r.at[k - 1],
                    seq=seq_at(k),
                ).start()
            return carry

        lax.fori_loop(0, feat_local // col_tile, body, 0)

    share_step = min(tiles + 1, steps)
    proj_step = min(tiles + 3, steps)

    def step(n, carry):
        @pl.when(n < steps)
        def _():
            c, i = n // tiles, lax.rem(n, tiles)

            @pl.when(n == 0)
            def _():
                for q in range(CORES):
                    for k in range(chips):
                        w_copy(0, q, k).wait()

            for cc in range(1, chunks):

                @pl.when(n == cc * tiles)
                def _():
                    for q in range(CORES):
                        for k in range(chips):
                            w_copy(cc, q, k).wait()

            @pl.when(c == 0)
            def _():
                scale_tile(i)

            part = jnp.dot(e_buf[ds(i, TILE), :], w_buf[c], preferred_element_type=F32)
            acc1[lax.rem(n, 2)] = part[:, :own_cols]
            s1[n] = part[:, own_cols:].astype(BF16)
            first(n).start()

            @pl.when(n == tiles - 1)
            def _():
                for k in range(1, mps):
                    sq_send(k).start()

        @pl.when(n == share_step)
        def _():
            for k in range(1, seqs):
                f_send(k).wait_recv()
                f_share(k).start()

        @pl.when(n > 0)
        def _():
            p = n - 1
            c, i = p // tiles, lax.rem(p, tiles)
            first(p).wait()
            total = acc1[lax.rem(p, 2)] + r1[p].astype(F32)
            acc2[c, ds(i, TILE), :] = total[:, :LANES]
            for k in range(1, chips):
                s2[p, k - 1] = total[:, k * LANES : (k + 1) * LANES].astype(BF16)
                second(p, k).start()

        @pl.when(n == proj_step)
        def _():
            project()

        return carry

    lax.fori_loop(0, steps + 1, step, 0)

    for k in range(1, mps):
        sq_send(k).wait()
    squares = sq_own[...]
    for k in range(1, mps):
        squares = squares + sq_recv[k - 1]
    scale[...] = mask[...] * lax.rsqrt(squares / width + 1e-05)

    def z_send(c, k):
        return remote(
            by_owner.at[c, ds(seq_at(k), block), :],
            arrived.at[c, ds(s, block), :],
            send_z.at[c, k - 1],
            recv_z.at[c, k - 1],
            seq=seq_at(k),
        )

    def out_at(rows, half, c):
        at = pl.ds(pl.multiple_of(half * cols + c * LANES, LANES), LANES)
        return slots_out.at[rows, at]

    def y_send(src, rows, c):
        return remote(src, out_at(rows, g, c), send_y.at[c], recv_y.at[c], group=peer)

    def local(src, rows, c):
        return pltpu.make_async_copy(src, out_at(rows, g, c), loc_sem.at[c])

    everything = pl.ds(0, slots * page)

    def finish(c):
        for i in range(tiles):
            for k in range(1, chips):
                second(c * tiles + i, k).wait()

        def body(b, carry):
            rows = ds(b, LANES)
            n = c * tiles + b // (TILE // LANES)
            within = ds(lax.rem(b, TILE // LANES), LANES)
            value = acc2[c, rows, :]
            for k in range(1, chips):
                value = value + r2[n, k - 1, within, :].astype(F32)
            acc2[c, rows, :] = value * spread_rows(scale[pl.ds(b, 1), :])
            return carry

        lax.fori_loop(0, tokens // LANES, body, 0)
        chosen = sel[...]
        for t in range(page):
            rows = acc2[c, pl.ds(t, pages, stride=page), :].astype(BF16)
            outf[pl.ds(t, slots, stride=page), :] = jnp.dot(
                chosen, rows, preferred_element_type=F32
            )
        by_owner[c] = outf[...].astype(BF16)
        for k in range(1, seqs):
            z_send(c, k).start()
        mine = ds(s, block)

        @pl.when(g == 0)
        def _():
            y_send(by_owner.at[c, mine, :], mine, c).start()
            local(by_owner.at[c], everything, c).start()

        @pl.when(g != 0)
        def _():
            y_send(by_owner.at[c], everything, c).start()
            local(by_owner.at[c, mine, :], mine, c).start()

    def forward(c, k):
        z_send(c, k).wait_recv()
        rows = ds(seq_from(k), block)

        @pl.when(g == 0)
        def _():
            y_send(arrived.at[c, rows, :], rows, c).start()

        @pl.when(g != 0)
        def _():
            local(arrived.at[c, rows, :], rows, c).start()

    finish(0)

    for k in range(1, seqs):
        p_copy(k).wait()
    own_rows = ds(g, half_rows)

    def gelu_body(t, carry):
        at = ds(t, col_tile)
        total = p_own[s, :, at] + bias[:, at].astype(F32)
        for k in range(1, seqs):
            total = total + p_recv[k - 1, :, at].astype(F32)
        hid[own_rows, at] = (
            0.5 * total * (1.0 + lax.erf(total * 0.5**0.5))
        ).astype(BF16)
        return carry

    lax.fori_loop(0, feat_local // col_tile, gelu_body, 0)
    h_send = remote(hid.at[own_rows, :], hid.at[own_rows, :], send_h, recv_h, group=peer)
    h_send.start()

    for c in range(1, chunks):
        finish(c)
    for k in range(1, seqs):
        forward(0, k)

    h_send.wait()
    hid_copy = pltpu.make_async_copy(hid, hid_out, misc_sem.at[1])
    hid_copy.start()
    total = jnp.zeros((rows_img, LANES), F32)
    for j in range(feat_local // LANES):
        at = slice(j * LANES, (j + 1) * LANES)
        value = hid[:, at].astype(F32)
        total = total + value * value
        i_scaled[:, at] = (value * gain[:, at].astype(F32)).astype(BF16)
    isq_own[...] = jnp.broadcast_to(
        jnp.sum(jnp.transpose(total), axis=0, keepdims=True), isq_own.shape
    )

    def iq_send(k):
        return remote(isq_own, isq_recv.at[k - 1], send_iq.at[k - 1], recv_iq.at[k - 1], mp=mp_at(k))

    for k in range(1, mps):
        iq_send(k).start()
    for c in range(chunks):
        part = jnp.dot(i_scaled[...], w_buf[c], preferred_element_type=F32)
        i_acc[c] = part[:, :own_cols]
        is1[c] = part[:, own_cols:].astype(BF16)
    i_first = remote(is1, ir1, send_i1, recv_i1, mp=partner)
    i_first.start()

    def i_second(k):
        return remote(
            is2.at[k - 1], ir2.at[k - 1], send_i2.at[k - 1], recv_i2.at[k - 1], mp=chip_at(k)
        )

    i_first.wait()
    for c in range(chunks):
        total = i_acc[c] + ir1[c].astype(F32)
        i_acc[c] = total
        for k in range(1, chips):
            is2[k - 1, c] = total[:, k * LANES : (k + 1) * LANES].astype(BF16)
    for k in range(1, chips):
        i_second(k).start()
    for k in range(1, mps):
        iq_send(k).wait()
    squares = isq_own[...]
    for k in range(1, mps):
        squares = squares + isq_recv[k - 1]
    i_scale = spread_rows(lax.rsqrt(squares / width + 1e-05)[:1])
    for k in range(1, chips):
        i_second(k).wait()
    for c in range(chunks):
        value = i_acc[c, :, :LANES]
        for k in range(1, chips):
            value = value + ir2[k - 1, c].astype(F32)
        ikv[:, c * LANES : (c + 1) * LANES] = (value * i_scale).astype(BF16)

    def img_at(index, half):
        return img_out.at[index, :, pl.ds(pl.multiple_of(half * cols, cols), cols)]

    def iz_send(k):
        return remote(ikv, img_at(s, g), send_iz.at[k - 1], recv_iz.at[k - 1], seq=seq_at(k))

    iy_send = remote(ikv, img_at(s, g), send_iy, recv_iy, group=peer)
    for k in range(1, seqs):
        iz_send(k).start()
    iy_send.start()
    i_local = pltpu.make_async_copy(ikv, img_at(s, g), misc_sem.at[2])
    i_local.start()

    def if_send(k):
        src = seq_from(k)
        return remote(
            img_at(src, 0), img_at(src, 0), send_if.at[k - 1], recv_if.at[k - 1], group=peer
        )

    for c in range(1, chunks):
        for k in range(1, seqs):
            forward(c, k)
    for k in range(1, seqs):
        iz_send(k).wait_recv()

        @pl.when(g == 0)
        def _():
            if_send(k).start()

    for c in range(chunks):
        for k in range(1, seqs):
            z_send(c, k).wait_send()
        y_send(by_owner.at[c], everything, c).wait()
        local(by_owner.at[c], everything, c).wait()
    for k in range(1, seqs):
        f_send(k).wait_send()
        d_send(k).wait()
        iz_send(k).wait_send()

        @pl.when(g == 0)
        def _():
            if_send(k).wait_send()

        @pl.when(g != 0)
        def _():
            if_send(k).wait_recv()

    iy_send.wait()
    i_local.wait()
    d_local.wait()
    hid_copy.wait()


def prefill(mesh_sizes, page, width, embeds, feats, proj_w, bias, gain, kv_w, sel, mask, dest):
    groups, seqs, mps = mesh_sizes
    chips = mps // CORES
    tokens, feat_local = embeds.shape
    tiles = tokens // TILE
    _, half_rows, channels = feats.shape
    rows_img = half_rows * groups
    block_cols = kv_w.shape[1] // mps
    cols = block_cols // groups
    chunks = cols // LANES
    steps = chunks * tiles
    slots = sel.shape[0]
    dma = pltpu.SemaphoreType.DMA
    vmem = pl.BlockSpec(memory_space=pltpu.VMEM)
    anywhere = pl.BlockSpec(memory_space=pl.ANY)
    dense = tokens // LANES
    return pl.pallas_call(
        functools.partial(prefill_kernel, groups, seqs, mps, page, width),
        out_shape=(
            jax.ShapeDtypeStruct((slots * page, block_cols), BF16),
            jax.ShapeDtypeStruct((rows_img, feat_local), BF16),
            jax.ShapeDtypeStruct((seqs, rows_img, block_cols), BF16),
            jax.ShapeDtypeStruct((seqs, 8, rows_img), F32),
        ),
        in_specs=[anywhere] * 3 + [vmem, vmem, anywhere, vmem, vmem, anywhere],
        out_specs=(anywhere,) * 4,
        scratch_shapes=[
            pltpu.VMEM((tokens, feat_local), BF16),
            pltpu.VMEM((chunks, feat_local, mps * LANES), BF16),
            pltpu.VMEM((channels, feat_local), BF16),
            pltpu.VMEM((seqs, half_rows, channels), BF16),
            pltpu.VMEM((2, TILE, chips * LANES), F32),
            pltpu.VMEM((steps, TILE, chips * LANES), BF16),
            pltpu.VMEM((steps, TILE, chips * LANES), BF16),
            pltpu.VMEM((chunks, tokens, LANES), F32),
            pltpu.VMEM((steps, chips - 1, TILE, LANES), BF16),
            pltpu.VMEM((steps, chips - 1, TILE, LANES), BF16),
            pltpu.VMEM((dense, LANES), F32),
            pltpu.VMEM((mps - 1, dense, LANES), F32),
            pltpu.VMEM((dense, LANES), F32),
            pltpu.VMEM((slots * page, LANES), F32),
            pltpu.VMEM((chunks, slots * page, LANES), BF16),
            pltpu.VMEM((chunks, slots * page, LANES), BF16),
            pltpu.VMEM((seqs, half_rows, feat_local), F32),
            pltpu.VMEM((seqs, half_rows, feat_local), BF16),
            pltpu.VMEM((seqs - 1, half_rows, feat_local), BF16),
            pltpu.VMEM((rows_img, feat_local), BF16),
            pltpu.VMEM((rows_img, feat_local), BF16),
            pltpu.VMEM((chunks, rows_img, chips * LANES), F32),
            pltpu.VMEM((chunks, rows_img, chips * LANES), BF16),
            pltpu.VMEM((chunks, rows_img, chips * LANES), BF16),
            pltpu.VMEM((chips - 1, chunks, rows_img, LANES), BF16),
            pltpu.VMEM((chips - 1, chunks, rows_img, LANES), BF16),
            pltpu.VMEM((8, LANES), F32),
            pltpu.VMEM((mps - 1, 8, LANES), F32),
            pltpu.VMEM((rows_img, cols), BF16),
            dma((1,)),
            dma((chunks, mps)),
            dma((tiles,)),
            dma,
            dma,
            dma((steps,)),
            dma((steps,)),
            dma((steps, chips - 1)),
            dma((steps, chips - 1)),
            dma((mps - 1,)),
            dma((mps - 1,)),
            dma((seqs - 1,)),
            dma((seqs - 1,)),
            dma((seqs - 1,)),
            dma((seqs - 1,)),
            dma((seqs - 1,)),
            dma((seqs - 1,)),
            dma,
            dma,
            dma,
            dma,
            dma((chips - 1,)),
            dma((chips - 1,)),
            dma((mps - 1,)),
            dma((mps - 1,)),
            dma((chunks, seqs - 1)),
            dma((chunks, seqs - 1)),
            dma((chunks,)),
            dma((chunks,)),
            dma((chunks,)),
            dma((seqs - 1,)),
            dma((seqs - 1,)),
            dma,
            dma,
            dma((seqs - 1,)),
            dma((seqs - 1,)),
            dma((seqs - 1,)),
            dma((seqs - 1,)),
            dma((3,)),
        ],
        compiler_params=pltpu.CompilerParams(
            collective_id=0, has_side_effects=True, vmem_limit_bytes=62 * 1024 * 1024
        ),
        name="prefill_pages",
    )(embeds, feats, proj_w, bias, gain, kv_w, sel, mask, dest)


def patch_kernel(index_ref, offset_ref, text, img, dest, out):
    rows = text.shape[0]
    first = offset_ref[pl.program_id(0)]
    spots = (dest[0, :1, :] - first.astype(F32)).astype(jnp.int32)
    hit = lax.broadcasted_iota(jnp.int32, (rows, dest.shape[2]), 0) == spots
    placed = jnp.dot(
        jnp.where(hit, 1.0, 0.0).astype(BF16), img[0], preferred_element_type=F32
    )
    out[...] = (text[...].astype(F32) + placed).astype(BF16)


def patch(index, offset, text, img, dest):
    seqs, rows_img, block_cols = img.shape
    block = text.shape[0] // seqs
    return pl.pallas_call(
        patch_kernel,
        out_shape=jax.ShapeDtypeStruct(text.shape, text.dtype),
        grid_spec=pltpu.PrefetchScalarGridSpec(
            num_scalar_prefetch=2,
            grid=(seqs,),
            in_specs=[
                pl.BlockSpec((block, block_cols), lambda b, index, offset: (b, 0)),
                pl.BlockSpec((1, rows_img, block_cols), lambda b, index, offset: (index[b], 0, 0)),
                pl.BlockSpec((1, 8, rows_img), lambda b, index, offset: (index[b], 0, 0)),
            ],
            out_specs=pl.BlockSpec((block, block_cols), lambda b, index, offset: (b, 0)),
        ),
        name="place_images",
    )(index, offset, text, img, dest)


def per_device(
    mesh_sizes,
    embeds,
    image_feats,
    image_pos,
    proj_w,
    proj_b,
    norm_gain,
    kv_w,
    prompt_lengths,
    page_owner,
    queries,
    kv_cache,
    new_kv,
    cache_lengths,
):
    groups, seqs, mps = mesh_sizes
    group_index = lax.axis_index("group")
    prefill_side = group_index == 0
    seq_index = lax.axis_index("seq")
    token_rows, width_local = embeds.shape
    width = width_local * mps
    image_rows, all_channels = image_feats.shape
    prompt_len = token_rows * seqs // prompt_lengths.shape[0]
    channels = proj_w.shape[0]

    half_rows = image_rows // groups
    features = lax.dynamic_slice_in_dim(image_feats, group_index * half_rows, half_rows, axis=0)
    feats = jnp.transpose(features.reshape(half_rows, seqs, channels), (1, 0, 2))

    pages_dev = page_owner.shape[0]
    page = token_rows // pages_dev
    capacity = 2 * pages_dev // seqs
    slots = seqs * capacity
    owners = page_owner[:, 0]
    earlier = jnp.arange(pages_dev)[None, :] < jnp.arange(pages_dev)[:, None]
    same = owners[:, None] == owners[None, :]
    page_rank = jnp.sum((earlier & same).astype(jnp.int32), axis=1)
    slot_index = owners * capacity + page_rank
    sel = (jnp.arange(slots, dtype=jnp.int32)[:, None] == slot_index[None, :]).astype(BF16)

    first = seq_index * token_rows
    positions = first + jnp.arange(token_rows, dtype=jnp.int32)
    is_live = live_rows(positions, prompt_lengths, prompt_len)
    is_image = jnp.any(positions[:, None] == image_pos[None, :], axis=1)
    mask = (is_live & ~is_image).astype(F32).reshape(token_rows // LANES, LANES)

    local_pos = image_pos - first
    on_page = (local_pos // page)[:, None] == jnp.arange(pages_dev, dtype=jnp.int32)[None, :]
    image_slot = jnp.sum(jnp.where(on_page, slot_index[None, :], 0), axis=1)
    image_live = live_rows(image_pos, prompt_lengths, prompt_len)
    dest = jnp.where(image_live, image_slot * page + local_pos % page, -(1 << 20))
    dest = jnp.broadcast_to(dest.astype(F32)[None, :], (8, image_rows))

    text, image_hidden, img, dest_all = prefill(
        mesh_sizes,
        page,
        width,
        embeds,
        feats,
        proj_w,
        proj_b[None, :],
        norm_gain[None, :],
        kv_w,
        sel,
        mask,
        dest,
    )
    order = jnp.arange(seqs, dtype=jnp.int32)
    index = jnp.where(prefill_side, seq_index, order)
    offset = jnp.where(prefill_side, order, seq_index) * (capacity * page)
    page_slots = patch(index, offset, text, img, dest_all)
    page_slots = page_slots.reshape(slots, page, text.shape[1])

    empty_rows = jnp.zeros(queries.shape, BF16)
    attended = gated(
        jnp.logical_not(prefill_side), attend, empty_rows, queries, kv_cache, new_kv, cache_lengths
    )
    row_states = jnp.where(prefill_side, image_hidden, attended)
    return (page_slots, row_states)


def solution(mesh):
    mesh_sizes = (mesh.shape["group"], mesh.shape["seq"], mesh.shape["mp"])
    in_specs = (
        P("seq", "mp"),
        P("seq", None),
        P("seq"),
        P("seq", "mp"),
        P("mp"),
        P("mp"),
        P("mp", None),
        P(),
        P("seq", None),
        P("seq", "mp"),
        P("seq", None, "mp"),
        P("seq", "mp"),
        P("seq"),
    )
    out_specs = (P(("group", "seq"), None, "mp"), P(("group", "seq"), "mp"))
    return jax.shard_map(
        functools.partial(per_device, mesh_sizes),
        mesh=mesh,
        in_specs=in_specs,
        out_specs=out_specs,
        check_vma=False,
    )
```

profile of v0, /device:TPU:28, one launch (start us, length us, event | category | flops | bytes accessed | tf_op | source)
XLA Modules:
  0.0 154.7 jit_solution(15298578044861104012)
XLA Ops:
  0.7 1.0 convert_reduce_fusion
  2.2 0.7 and_select_fusion.2
  2.9 0.7 fusion.54
  3.8 0.7 fusion.57
  5.1 1.3 broadcast_in_dim.95.bias
  6.4 1.3 broadcast_in_dim.96.gain
  7.7 0.7 fusion.46
  8.4 1.3 compare_reduce_fusion
  10.4 0.6 fusion.44.sel
  11.0 17.2 %conditional.1 = (bf16[128,2048]{1,0:T(8,128)(2,1)S(1)}) conditional(s32[]{:T(128)} %convert_element_type.52, () %tuple.14, (s32[128]{0:T(128)}, bf16[128,2048]{1,0:T(8,128)(2,1)}, bf16[128,128,512]{2,1,0:T(8,128)(2,1)}, bf16[128,512]{1,0:T(8,128)(2,1)}) %tuple.15), branch_computations={%region_5.6_spmd, %region_6.11_spmd} | conditional | flops 138737664 | bytes 93688360 | solution.py:20
  11.0 0.7 iota_compare_fusion
  11.8 1.0 slice_bitcast_fusion.3
  12.7 1.2 slice_bitcast_fusion.1
  14.7 5.2 %fusion.58 = (f32[128,8]{1,0:T(8,128)S(1)}, f32[128,8,128]{2,1,0:T(8,128)S(1)}) fusion(bf16[128,8,128]{2,1,0:T(8,128)(2,1)S(1)} %bitcast.43, bf16[128,128,512]{2,1,0:T(8,128)(2,1)} %get-tuple-element.31, pred[128,128]{1,0:T(8,128)(4,1)S(1)} %iota_compare_fusion), kind=kOutput, calls=%fused_computation.97 | convolution fusion | flops 33946624 | bytes 5001216 | tf_op jit(solution)/shard_map/cond/branch_1_fun/rqh,rjh->rqj/dot_general | solution.py:24
  20.3 3.5 %fusion.26 = bf16[128,8,128]{2,1,0:T(8,128)(2,1)S(1)} fusion(bf16[128,128,512]{2,1,0:T(8,128)(2,1)} %get-tuple-element.31, f32[128,8,128]{2,1,0:T(8,128)S(1)} %get-tuple-element.44, f32[128,128]{1,0:T(8,128)S(1)} %get-tuple-element.42, f32[128,8]{1,0:T(8,128)S(1)} %convert_element_type.40, f32[128,8]{1,0:T(8,128)S(1)} %get-tuple-element.37, ...), kind=kOutput, calls=%fused_computation.14 | convolution fusion | flops 34340864 | bytes 5058560 | tf_op jit(solution)/shard_map/cond/branch_1_fun/rqj,rjh->rqh/dot_general | solution.py:39
  23.8 2.4 %fusion.59 = (f32[128,8]{1,0:T(8,128)S(1)}, f32[128,8,128]{2,1,0:T(8,128)S(1)}) fusion(bf16[128,8,128]{2,1,0:T(8,128)(2,1)S(1)} %bitcast.41, bf16[128,128,512]{2,1,0:T(8,128)(2,1)S(1)} %copy-done.1, pred[128,128]{1,0:T(8,128)(4,1)S(1)} %iota_compare_fusion), kind=kOutput, calls=%fused_computation.98 | convolution fusion | flops 33946624 | bytes 5001216 | tf_op jit(solution)/shard_map/cond/branch_1_fun/rqh,rjh->rqj/dot_general | solution.py:24
  26.6 1.3 fusion.29
  28.2 0.8 copy-done.2
  29.0 1.0 constant_dynamic-slice_fusion
  30.0 2.7 %reshape.88 = bf16[64,4,1824]{2,1,0:T(4,128)(2,1)S(1)} reshape(bf16[64,7296]{1,0:T(8,128)(2,1)} %constant_dynamic-slice_fusion) | data formatting | bytes 1867776 | tf_op jit(solution)/shard_map/reshape | solution.py:768
  32.7 1.0 copy.36
  33.7 112.7 %prefill_pages.1 = (bf16[4096,512]{1,0:T(8,128)(2,1)}, bf16[128,2048]{1,0:T(8,128)(2,1)}, bf16[4,128,512]{2,1,0:T(8,128)(2,1)}, f32[4,8,128]{2,1,0:T(8,128)}) custom-call(bf16[2048,2048]{1,0:T(8,128)(2,1)} %embeds.1, bf16[4,64,1824]{2,1,0:T(8,128)(2,1)} %bitcast.39, bf16[1824,2048]{1,0:T(8,128)(2,1)} %proj_w.1, bf16[1,2048]{1,0:T(2,128)(2,1)} %broadcast_in_dim.95.bias, ...), custom_call_target="tpu_custom_call" | custom-call | tf_op jit(solution)/shard_map/prefill_pages/pallas_call | solution.py:622
  146.4 1.9 %broadcast_select_fusion = bf16[128,2048]{1,0:T(8,128)(2,1)} fusion(bf16[128,2048]{1,0:T(8,128)(2,1)} %get-tuple-element.24, bf16[128,2048]{1,0:T(8,128)(2,1)} %copy-done.2, pred[]{:T(512)S(6)} %eq.40), kind=kLoop, calls=%fused_computation.50 | loop fusion | flops 262144 | bytes 1572865 | tf_op jit(solution)/shard_map/jit(_where)/select_n | solution.py:818
  148.3 6.3 %place_images.1 = bf16[4096,512]{1,0:T(8,128)(2,1)} custom-call(s32[4]{0:T(128)} %get-tuple-element.51.index_ref, s32[4]{0:T(128)} %get-tuple-element.52.offset_ref, bf16[4096,512]{1,0:T(8,128)(2,1)} %get-tuple-element.21.text, bf16[4,128,512]{2,1,0:T(8,128)(2,1)} %get-tuple-element.22.img, f32[4,8,128]{2,1,0:T(8,128)} %get-tuple-element.23.dest), custom_call_target="tpu_custom_call" | custom-call | tf_op jit(solution)/shard_map/place_images/pallas_call | solution.py:723
  (24 shorter events, 3.7 us)
Async XLA Ops:
  0.6 28.4 %copy-start = (bf16[128,7296]{1,0:T(8,128)(2,1)S(1)}, bf16[128,7296]{1,0:T(8,128)(2,1)}, u32[]{:S(2)}) copy-start(bf16[128,7296]{1,0:T(8,128)(2,1)} %param.16) | copy-start | bytes 5603332
  11.7 12.1 %copy-start.1 = (bf16[128,128,512]{2,1,0:T(8,128)(2,1)S(1)}, bf16[128,128,512]{2,1,0:T(8,128)(2,1)}, u32[]{:S(2)}) copy-start(bf16[128,128,512]{2,1,0:T(8,128)(2,1)} %get-tuple-element.31) | copy-start | bytes 50331652 | tf_op jit(solution)/shard_map/cond
  28.2 0.8 copy-start.2
where the time goes:
time: 155 us
  Pallas kernels  119 us (77%)
  matrix products  12.8 us (8%)
  other arithmetic  11.7 us (8%)
  local copies, waits for them, and re-layouts  10.1 us (7%)
    pallas_call x1, Pallas kernels, prefill(): pl.pallas_call(functools.partial(prefill_kernel, groups, seqs, mps, page,...  113 us
    dot_general x2, matrix products, attend_head(): jnp.einsum('rqh,rjh->rqj', queries, keys, preferred_element_type=jnp.floa...  7.54 us
    pallas_call x1, Pallas kernels, patch(): pl.pallas_call(patch_kernel, out_shape=jax.ShapeDtypeStruct(text.shape, t...  6.31 us
    dot_general x2, matrix products, attend_head(): jnp.einsum('rqj,rjh->rqh', probability, values, preferred_element_type=jn...  4.75 us
    reshape x2, local copies, waits for them, and re-layouts, per_device(): features.reshape(half_rows, seqs, channels)  3.72 us

commit v1 on v0

--- a/solution.py
+++ b/solution.py
@@ -16,58 +16,6 @@
 BF16 = jnp.bfloat16
 
 
-def gated(condition, action, empty_value, *operands):
-    return lax.cond(condition, action, lambda *unused: empty_value, *operands)
-
-
-def attend_head(queries, keys, values, fresh_key, fresh_value, in_cache):
-    scores = jnp.einsum(
-        "rqh,rjh->rqj", queries, keys, preferred_element_type=jnp.float32
-    ) * HEAD ** (-0.5)
-    scores = jnp.where(in_cache[:, None, :], scores, -1e30)
-    own_score = jnp.einsum(
-        "rqh,rh->rq", queries, fresh_key, preferred_element_type=jnp.float32
-    ) * HEAD ** (-0.5)
-    row_max = jnp.maximum(jnp.max(scores, axis=2), own_score)
-    weights = jnp.exp(scores - row_max[..., None])
-    own_weight = jnp.exp(own_score - row_max)
-    denominator = jnp.sum(weights, axis=2) + own_weight
-    probability = (weights / denominator[..., None]).astype(jnp.bfloat16)
-    own_prob = lax.optimization_barrier((own_weight / denominator).astype(jnp.bfloat16)).astype(
-        jnp.float32
-    )
-    attended = jnp.einsum("rqj,rjh->rqh", probability, values, preferred_element_type=jnp.float32)
-    attended = attended + own_prob[..., None] * fresh_value[:, None, :].astype(jnp.float32)
-    return attended.astype(jnp.bfloat16)
-
-
-def attend(queries, kv_cache, new_kv, cache_lengths):
-    row_count = queries.shape[0]
-    heads_kv = kv_cache.shape[2] // (2 * HEAD)
-    share = queries.shape[1] // heads_kv
-    in_cache = jnp.arange(kv_cache.shape[1], dtype=jnp.int32)[None, :] < cache_lengths[:, None]
-    heads = []
-    for head in range(heads_kv):
-        key, value, end = 2 * HEAD * head, 2 * HEAD * head + HEAD, 2 * HEAD * (head + 1)
-        attended = attend_head(
-            queries[:, head * share : (head + 1) * share].reshape(row_count, share // HEAD, HEAD),
-            kv_cache[:, :, key:value],
-            kv_cache[:, :, value:end],
-            new_kv[:, key:value],
-            new_kv[:, value:end],
-            in_cache,
-        )
-        heads.append(attended.reshape(row_count, share))
-    return jnp.concatenate(heads, axis=1)
-
-
-def live_rows(positions, prompt_lengths, prompt_len):
-    prompt_ids = positions // prompt_len
-    match = prompt_ids[..., None] == jnp.arange(prompt_lengths.shape[0], dtype=jnp.int32)
-    limit = jnp.sum(jnp.where(match, prompt_lengths, 0), axis=-1)
-    return positions % prompt_len < limit
-
-
 def ds(index, size):
     return pl.ds(pl.multiple_of(index * size, size), size)
 
@@ -80,21 +28,29 @@
     groups,
     seqs,
     mps,
-    page,
-    width,
+    prompt_len,
     embeds,
-    feats,
+    image_feats,
     proj_w,
+    kv_w,
+    kv_cache,
+    image_pos,
     bias,
     gain,
-    kv_w,
+    page_owner,
+    queries,
+    new_kv,
+    cache_lengths,
+    prompt_lengths,
+    slots_out,
+    states_out,
+    img_out,
+    dest_out,
     sel,
     mask,
     dest,
-    slots_out,
-    hid_out,
-    img_out,
-    dest_out,
+    f_rows,
+    feats,
     e_buf,
     w_buf,
     pw_buf,
@@ -111,6 +67,9 @@
     outf,
     by_owner,
     arrived,
+    kv_send,
+    kv_recv,
+    by_peer,
     p_own,
     p_send,
     p_recv,
@@ -124,7 +83,18 @@
     isq_own,
     isq_recv,
     ikv,
+    q_rows,
+    fresh,
+    lengths,
+    cache,
+    a_scores,
+    a_keys,
+    a_values,
+    a_limits,
+    a_rows,
+    attended,
     load_sem,
+    cache_sem,
     w_sem,
     e_sem,
     pw_sem,
@@ -153,7 +123,10 @@
     recv_z,
     send_y,
     recv_y,
+    send_k,
+    recv_k,
     loc_sem,
+    loc2_sem,
     send_iz,
     recv_iz,
     send_iy,
@@ -181,8 +154,11 @@
     core_rows = half_rows // CORES
     cols = chunks * LANES
     block_cols = cols * groups
-    slots = sel.shape[0]
-    pages = sel.shape[1]
+    slots, pages = sel.shape
+    page = tokens // pages
+    capacity = slots // seqs
+    width = feat_local * mps
+    channels = feats.shape[2]
     block = slots * page // seqs
     own_cols = chips * LANES
 
@@ -220,6 +196,14 @@
             w_sem.at[c, q * chips + k],
         )
 
+    f_load = pltpu.make_async_copy(image_feats.at[ds(g, half_rows), :], f_rows, load_sem.at[0])
+    f_load.start()
+    barrier = pltpu.get_barrier_semaphore()
+    for k in range(1, seqs):
+        pl.semaphore_signal(barrier, inc=1, device_id={"seq": seq_at(k)}, device_id_type=MESH)
+    for k in range(1, mps):
+        pl.semaphore_signal(barrier, inc=1, device_id={"mp": mp_at(k)}, device_id_type=MESH)
+    pl.semaphore_signal(barrier, inc=1, device_id={"group": peer}, device_id_type=MESH)
     e_copy(0).start()
     for q in range(CORES):
         for k in range(chips):
@@ -232,15 +216,13 @@
                 w_copy(c, q, k).start()
     pw_copy = pltpu.make_async_copy(proj_w, pw_buf, pw_sem)
     pw_copy.start()
+
+    f_load.wait()
+    for b in range(seqs):
+        feats[b] = f_rows[:, b * channels : (b + 1) * channels]
     own_feats = pltpu.make_async_copy(feats.at[s], f_buf.at[s], fl_sem)
     own_feats.start()
 
-    barrier = pltpu.get_barrier_semaphore()
-    for k in range(1, seqs):
-        pl.semaphore_signal(barrier, inc=1, device_id={"seq": seq_at(k)}, device_id_type=MESH)
-    for k in range(1, mps):
-        pl.semaphore_signal(barrier, inc=1, device_id={"mp": mp_at(k)}, device_id_type=MESH)
-    pl.semaphore_signal(barrier, inc=1, device_id={"group": peer}, device_id_type=MESH)
     pl.semaphore_wait(barrier, seqs - 1 + mps - 1 + 1)
 
     def f_send(k):
@@ -269,6 +251,40 @@
 
     for k in range(1, seqs):
         f_send(k).start()
+
+    prompt = (s * tokens) // prompt_len
+    limit = prompt_lengths[prompt]
+    base = s * tokens - prompt * prompt_len
+    spots = image_pos[...] - s * tokens
+    down = lax.broadcasted_iota(jnp.int32, (pages, LANES), 0)
+    across = lax.broadcasted_iota(jnp.int32, (pages, LANES), 1)
+    owner_down = jnp.broadcast_to(page_owner[...].astype(F32), (pages, LANES))
+    owner_across = jnp.transpose(owner_down)
+    rank = jnp.sum(
+        jnp.where((owner_down == owner_across) & (down < across), 1.0, 0.0), axis=0, keepdims=True
+    )
+    slot = owner_across[:1] * capacity + rank
+    slot_rows = lax.broadcasted_iota(jnp.int32, (slots, LANES), 0).astype(F32)
+    sel[...] = jnp.where(slot_rows == slot, 1.0, 0.0).astype(BF16)
+    page_bits = page.bit_length() - 1
+    on_page = down == lax.shift_right_logical(spots, page_bits)
+    image_slot = jnp.sum(jnp.where(on_page, spread_rows(slot), 0.0), axis=0, keepdims=True)
+    image_row = image_slot * page + (spots & (page - 1)).astype(F32)
+    dest[...] = jnp.broadcast_to(
+        jnp.where(spots + base < limit, image_row, -1048576.0), dest.shape
+    )
+    dense = mask.shape[0]
+    tall = lax.broadcasted_iota(jnp.int32, (dense, LANES), 0)
+    image_block = jnp.where(tall == lax.shift_right_logical(spots, 7), 1.0, 0.0)
+    image_lane = jnp.where(down == (spots & (LANES - 1)), 1.0, 0.0)
+    images = lax.dot_general(
+        image_block.astype(BF16),
+        image_lane.astype(BF16),
+        (((1,), (1,)), ((), ())),
+        preferred_element_type=F32,
+    )
+    token = tall * LANES + lax.broadcasted_iota(jnp.int32, (dense, LANES), 1)
+    mask[...] = jnp.where((token + base < limit) & (images < 0.5), 1.0, 0.0)
     for k in range(1, seqs):
         d_send(k).start()
     d_local = pltpu.make_async_copy(dest, dest_out.at[s], misc_sem.at[0])
@@ -424,6 +440,23 @@
 
     everything = pl.ds(0, slots * page)
 
+    def select(c, target):
+        chosen = sel[...]
+        for t in range(page):
+            rows = acc2[c, pl.ds(t, pages, stride=page), :].astype(BF16)
+            outf[pl.ds(t, slots, stride=page), :] = jnp.dot(
+                chosen, rows, preferred_element_type=F32
+            )
+        target[c] = outf[...].astype(BF16)
+
+    def k_send(c):
+        return remote(kv_send.at[c], kv_recv.at[c], send_k.at[c], recv_k.at[c], group=peer)
+
+    def local2(c):
+        return pltpu.make_async_copy(
+            by_peer.at[c], out_at(everything, 1 - g, c), loc2_sem.at[c]
+        )
+
     def finish(c):
         for i in range(tiles):
             for k in range(1, chips):
@@ -436,17 +469,13 @@
             value = acc2[c, rows, :]
             for k in range(1, chips):
                 value = value + r2[n, k - 1, within, :].astype(F32)
-            acc2[c, rows, :] = value * spread_rows(scale[pl.ds(b, 1), :])
+            value = value * spread_rows(scale[pl.ds(b, 1), :])
+            acc2[c, rows, :] = value
+            kv_send[c, rows, :] = value.astype(BF16)
             return carry
 
         lax.fori_loop(0, tokens // LANES, body, 0)
-        chosen = sel[...]
-        for t in range(page):
-            rows = acc2[c, pl.ds(t, pages, stride=page), :].astype(BF16)
-            outf[pl.ds(t, slots, stride=page), :] = jnp.dot(
-                chosen, rows, preferred_element_type=F32
-            )
-        by_owner[c] = outf[...].astype(BF16)
+        select(c, by_owner)
         for k in range(1, seqs):
             z_send(c, k).start()
         mine = ds(s, block)
@@ -458,8 +487,13 @@
 
         @pl.when(g != 0)
         def _():
-            y_send(by_owner.at[c], everything, c).start()
             local(by_owner.at[c, mine, :], mine, c).start()
+
+    def take_peer(c):
+        k_send(c).wait_recv()
+        acc2[c] = kv_recv[c].astype(F32)
+        select(c, by_peer)
+        local2(c).start()
 
     def forward(c, k):
         z_send(c, k).wait_recv()
@@ -493,14 +527,28 @@
     h_send = remote(hid.at[own_rows, :], hid.at[own_rows, :], send_h, recv_h, group=peer)
     h_send.start()
 
+
+    @pl.when(g != 0)
+    def _():
+        k_send(0).start()
+
     for c in range(1, chunks):
         finish(c)
-    for k in range(1, seqs):
-        forward(0, k)
+    forward(0, 1)
 
     h_send.wait()
-    hid_copy = pltpu.make_async_copy(hid, hid_out, misc_sem.at[1])
-    hid_copy.start()
+
+    @pl.when(g != 0)
+    def _():
+        for c in range(1, chunks):
+            k_send(c).start()
+
+    hid_copy = pltpu.make_async_copy(hid, states_out, misc_sem.at[1])
+
+    @pl.when(g == 0)
+    def _():
+        hid_copy.start()
+
     total = jnp.zeros((rows_img, LANES), F32)
     for j in range(feat_local // LANES):
         at = slice(j * LANES, (j + 1) * LANES)
@@ -569,6 +617,96 @@
             img_at(src, 0), img_at(src, 0), send_if.at[k - 1], recv_if.at[k - 1], group=peer
         )
 
+    heads = queries.shape[1] // HEAD
+    kv_heads = kv_cache.shape[2] // (2 * HEAD)
+    share = heads // kv_heads
+    rows_dec = queries.shape[0]
+    batch = LANES // heads
+
+    def cache_copy(b):
+        return pltpu.make_async_copy(
+            kv_cache.at[ds(b, batch)], cache.at[lax.rem(b, 2)], cache_sem.at[lax.rem(b, 2)]
+        )
+
+    def attend_batch(b, carry):
+        cache_copy(b).wait()
+
+        @pl.when(b + 1 < rows_dec // batch)
+        def _():
+            cache_copy(b + 1).start()
+
+        at = lax.rem(b, 2)
+        for r in range(batch):
+            span = slice(r * heads, (r + 1) * heads)
+            query = q_rows[pl.ds(pl.multiple_of(b * LANES + r * heads, 8), heads), :].astype(BF16)
+            new = fresh[pl.ds(b * batch + r, 1), :]
+            a_limits[span, :] = jnp.broadcast_to(
+                lengths[pl.ds(b * batch + r, 1), :], (heads, LANES)
+            )
+            for h in range(kv_heads):
+                part = slice(r * heads + h * share, r * heads + (h + 1) * share)
+                key = 2 * HEAD * h
+                product = lax.dot_general(
+                    query,
+                    cache[at, r, :, key : key + HEAD],
+                    (((1,), (1,)), ((), ())),
+                    preferred_element_type=F32,
+                )
+                a_scores[part, :] = product[h * share : (h + 1) * share]
+                a_keys[part, :] = jnp.broadcast_to(new[:, key : key + HEAD], (share, HEAD))
+                a_values[part, :] = jnp.broadcast_to(
+                    new[:, key + HEAD : key + 2 * HEAD], (share, HEAD)
+                )
+        lane = lax.broadcasted_iota(jnp.int32, (LANES, LANES), 1).astype(F32)
+        scores = jnp.where(lane < a_limits[...], a_scores[...] * HEAD ** (-0.5), -1e30)
+        own = jnp.sum(q_rows[ds(b, LANES), :] * a_keys[...], axis=1, keepdims=True) * HEAD ** (-0.5)
+        top = jnp.maximum(jnp.max(scores, axis=1, keepdims=True), own)
+        weights = jnp.exp(scores - top)
+        own_weight = jnp.exp(own - top)
+        total = jnp.sum(weights, axis=1, keepdims=True) + own_weight
+        a_scores[...] = weights / total
+        own_part = (own_weight / total).astype(BF16).astype(F32) * a_values[...]
+        a_values[...] = own_part
+        for r in range(batch):
+            span = slice(r * heads, (r + 1) * heads)
+            probs = a_scores[span, :].astype(BF16)
+            for h in range(kv_heads):
+                part = slice(r * heads + h * share, r * heads + (h + 1) * share)
+                value = 2 * HEAD * h + HEAD
+                product = jnp.dot(
+                    probs, cache[at, r, :, value : value + HEAD], preferred_element_type=F32
+                )
+                a_rows[pl.ds(pl.multiple_of(b * LANES, LANES) + r * heads + h * share, share), :] = (
+                    product[h * share : (h + 1) * share] + a_values[part, :]
+                )
+        return carry
+
+    att_copy = pltpu.make_async_copy(attended, states_out, misc_sem.at[1])
+
+    @pl.when(g != 0)
+    def _():
+        cache_copy(0).start()
+        for j in range(heads):
+            q_rows[pl.ds(j, rows_dec, stride=heads), :] = queries[
+                :, j * HEAD : (j + 1) * HEAD
+            ].astype(F32)
+        fresh[...] = new_kv[...].astype(F32)
+        lengths[...] = spread_rows(cache_lengths[...].astype(F32))
+        lax.fori_loop(0, rows_dec // batch, attend_batch, 0)
+        for j in range(heads):
+            attended[:, j * HEAD : (j + 1) * HEAD] = a_rows[
+                pl.ds(j, rows_dec, stride=heads), :
+            ].astype(BF16)
+        att_copy.start()
+
+    for k in range(2, seqs):
+        forward(0, k)
+
+    @pl.when(g == 0)
+    def _():
+        for c in range(chunks):
+            take_peer(c)
+
     for c in range(1, chunks):
         for k in range(1, seqs):
             forward(c, k)
@@ -582,8 +720,18 @@
     for c in range(chunks):
         for k in range(1, seqs):
             z_send(c, k).wait_send()
-        y_send(by_owner.at[c], everything, c).wait()
         local(by_owner.at[c], everything, c).wait()
+
+        @pl.when(g == 0)
+        def _():
+            y_send(by_owner.at[c], everything, c).wait_send()
+            local2(c).wait()
+
+        @pl.when(g != 0)
+        def _():
+            y_send(by_owner.at[c], everything, c).wait_recv()
+            k_send(c).wait_send()
+
     for k in range(1, seqs):
         f_send(k).wait_send()
         d_send(k).wait()
@@ -603,33 +751,60 @@
     hid_copy.wait()
 
 
-def prefill(mesh_sizes, page, width, embeds, feats, proj_w, bias, gain, kv_w, sel, mask, dest):
+def prefill(
+    mesh_sizes,
+    prompt_len,
+    embeds,
+    image_feats,
+    proj_w,
+    kv_w,
+    kv_cache,
+    image_pos,
+    bias,
+    gain,
+    page_owner,
+    queries,
+    new_kv,
+    cache_lengths,
+    prompt_lengths,
+):
     groups, seqs, mps = mesh_sizes
     chips = mps // CORES
     tokens, feat_local = embeds.shape
     tiles = tokens // TILE
-    _, half_rows, channels = feats.shape
-    rows_img = half_rows * groups
+    rows_img, all_channels = image_feats.shape
+    half_rows = rows_img // groups
+    channels = proj_w.shape[0]
     block_cols = kv_w.shape[1] // mps
     cols = block_cols // groups
     chunks = cols // LANES
     steps = chunks * tiles
-    slots = sel.shape[0]
+    pages = page_owner.shape[0]
+    page = tokens // pages
+    slots = seqs * (2 * pages // seqs)
+    rows_dec = queries.shape[0]
+    heads = queries.shape[1] // HEAD
+    batch = LANES // heads
     dma = pltpu.SemaphoreType.DMA
     vmem = pl.BlockSpec(memory_space=pltpu.VMEM)
     anywhere = pl.BlockSpec(memory_space=pl.ANY)
     dense = tokens // LANES
     return pl.pallas_call(
-        functools.partial(prefill_kernel, groups, seqs, mps, page, width),
+        functools.partial(prefill_kernel, groups, seqs, mps, prompt_len),
         out_shape=(
             jax.ShapeDtypeStruct((slots * page, block_cols), BF16),
             jax.ShapeDtypeStruct((rows_img, feat_local), BF16),
             jax.ShapeDtypeStruct((seqs, rows_img, block_cols), BF16),
             jax.ShapeDtypeStruct((seqs, 8, rows_img), F32),
         ),
-        in_specs=[anywhere] * 3 + [vmem, vmem, anywhere, vmem, vmem, anywhere],
+        in_specs=[anywhere] * 5 + [vmem] * 7 + [pl.BlockSpec(memory_space=pltpu.SMEM)],
         out_specs=(anywhere,) * 4,
         scratch_shapes=[
+            pltpu.VMEM((slots, pages), BF16),
+            pltpu.VMEM((dense, LANES), F32),
+            pltpu.VMEM((8, rows_img), F32),
+            pltpu.VMEM((half_rows, all_channels), BF16),
+            pltpu.VMEM((seqs, half_rows, channels), BF16),
             pltpu.VMEM((tokens, feat_local), BF16),
             pltpu.VMEM((chunks, feat_local, mps * LANES), BF16),
             pltpu.VMEM((channels, feat_local), BF16),
@@ -646,6 +821,9 @@
             pltpu.VMEM((slots * page, LANES), F32),
             pltpu.VMEM((chunks, slots * page, LANES), BF16),
             pltpu.VMEM((chunks, slots * page, LANES), BF16),
+            pltpu.VMEM((chunks, tokens, LANES), BF16),
+            pltpu.VMEM((chunks, tokens, LANES), BF16),
+            pltpu.VMEM((chunks, slots * page, LANES), BF16),
             pltpu.VMEM((seqs, half_rows, feat_local), F32),
             pltpu.VMEM((seqs, half_rows, feat_local), BF16),
             pltpu.VMEM((seqs - 1, half_rows, feat_local), BF16),
@@ -659,7 +837,18 @@
             pltpu.VMEM((8, LANES), F32),
             pltpu.VMEM((mps - 1, 8, LANES), F32),
             pltpu.VMEM((rows_img, cols), BF16),
+            pltpu.VMEM((rows_dec * heads, HEAD), F32),
+            pltpu.VMEM(new_kv.shape, F32),
+            pltpu.VMEM((rows_dec, LANES), F32),
+            pltpu.VMEM((2, batch) + kv_cache.shape[1:], BF16),
+            pltpu.VMEM((LANES, LANES), F32),
+            pltpu.VMEM((LANES, LANES), F32),
+            pltpu.VMEM((LANES, LANES), F32),
+            pltpu.VMEM((LANES, LANES), F32),
+            pltpu.VMEM((rows_dec * heads, HEAD), F32),
+            pltpu.VMEM(queries.shape, BF16),
             dma((1,)),
+            dma((2,)),
             dma((chunks, mps)),
             dma((tiles,)),
             dma,
@@ -689,6 +878,9 @@
             dma((chunks,)),
             dma((chunks,)),
             dma((chunks,)),
+            dma((chunks,)),
+            dma((chunks,)),
+            dma((chunks,)),
             dma((seqs - 1,)),
             dma((seqs - 1,)),
             dma,
@@ -703,7 +895,21 @@
             collective_id=0, has_side_effects=True, vmem_limit_bytes=62 * 1024 * 1024
         ),
         name="prefill_pages",
-    )(embeds, feats, proj_w, bias, gain, kv_w, sel, mask, dest)
+    )(
+        embeds,
+        image_feats,
+        proj_w,
+        kv_w,
+        kv_cache,
+        image_pos,
+        bias,
+        gain,
+        page_owner,
+        queries,
+        new_kv,
+        cache_lengths,
+        prompt_lengths,
+    )
 
 
 def patch_kernel(index_ref, offset_ref, text, img, dest, out):
@@ -758,64 +964,31 @@
     prefill_side = group_index == 0
     seq_index = lax.axis_index("seq")
     token_rows, width_local = embeds.shape
-    width = width_local * mps
-    image_rows, all_channels = image_feats.shape
     prompt_len = token_rows * seqs // prompt_lengths.shape[0]
-    channels = proj_w.shape[0]
-
-    half_rows = image_rows // groups
-    features = lax.dynamic_slice_in_dim(image_feats, group_index * half_rows, half_rows, axis=0)
-    feats = jnp.transpose(features.reshape(half_rows, seqs, channels), (1, 0, 2))
-
-    pages_dev = page_owner.shape[0]
-    page = token_rows // pages_dev
-    capacity = 2 * pages_dev // seqs
-    slots = seqs * capacity
-    owners = page_owner[:, 0]
-    earlier = jnp.arange(pages_dev)[None, :] < jnp.arange(pages_dev)[:, None]
-    same = owners[:, None] == owners[None, :]
-    page_rank = jnp.sum((earlier & same).astype(jnp.int32), axis=1)
-    slot_index = owners * capacity + page_rank
-    sel = (jnp.arange(slots, dtype=jnp.int32)[:, None] == slot_index[None, :]).astype(BF16)
-
-    first = seq_index * token_rows
-    positions = first + jnp.arange(token_rows, dtype=jnp.int32)
-    is_live = live_rows(positions, prompt_lengths, prompt_len)
-    is_image = jnp.any(positions[:, None] == image_pos[None, :], axis=1)
-    mask = (is_live & ~is_image).astype(F32).reshape(token_rows // LANES, LANES)
-
-    local_pos = image_pos - first
-    on_page = (local_pos // page)[:, None] == jnp.arange(pages_dev, dtype=jnp.int32)[None, :]
-    image_slot = jnp.sum(jnp.where(on_page, slot_index[None, :], 0), axis=1)
-    image_live = live_rows(image_pos, prompt_lengths, prompt_len)
-    dest = jnp.where(image_live, image_slot * page + local_pos % page, -(1 << 20))
-    dest = jnp.broadcast_to(dest.astype(F32)[None, :], (8, image_rows))
-
-    text, image_hidden, img, dest_all = prefill(
+    page = token_rows // page_owner.shape[0]
+    capacity = 2 * page_owner.shape[0] // seqs
+    text, row_states, img, dest_all = prefill(
         mesh_sizes,
-        page,
-        width,
+        prompt_len,
         embeds,
-        feats,
+        image_feats,
         proj_w,
+        kv_w,
+        kv_cache,
+        image_pos[None, :],
         proj_b[None, :],
         norm_gain[None, :],
-        kv_w,
-        sel,
-        mask,
-        dest,
+        page_owner,
+        queries,
+        new_kv,
+        cache_lengths[None, :],
+        prompt_lengths,
     )
     order = jnp.arange(seqs, dtype=jnp.int32)
     index = jnp.where(prefill_side, seq_index, order)
     offset = jnp.where(prefill_side, order, seq_index) * (capacity * page)
     page_slots = patch(index, offset, text, img, dest_all)
-    page_slots = page_slots.reshape(slots, page, text.shape[1])
-
-    empty_rows = jnp.zeros(queries.shape, BF16)
-    attended = gated(
-        jnp.logical_not(prefill_side), attend, empty_rows, queries, kv_cache, new_kv, cache_lengths
-    )
-    row_states = jnp.where(prefill_side, image_hidden, attended)
+    page_slots = page_slots.reshape(-1, page, text.shape[1])
     return (page_slots, row_states)
 
 

time: 155 us -> 124 us (0.80)
  the two profiles are of different devices: /device:TPU:28 before, /device:TPU:0 now
where the time goes in v1:
time: 124 us; the launch traced here: 122 us
  Pallas kernels  116 us (94%)
  local copies, waits for them, and re-layouts  4.76 us (4%)
    pallas_call x1, Pallas kernels, prefill(): pl.pallas_call(functools.partial(prefill_kernel, groups, seqs, mps, promp...  110 us
    pallas_call x1, Pallas kernels, patch(): pl.pallas_call(patch_kernel, out_shape=jax.ShapeDtypeStruct(text.shape, t...  6.39 us

profile of v1, /device:TPU:0, one launch (start us, length us, event | category | flops | bytes accessed | tf_op | source)
XLA Modules:
  0.0 122.1 jit_solution(8231111706654728410)
XLA Ops:
  0.6 0.5 broadcast_select_fusion.1
  1.2 1.3 %broadcast_in_dim.20.bias = bf16[1,2048]{1,0:T(2,128)(2,1)} reshape(bf16[2048]{0:T(1024)(128)(2,1)} %param.17) | data formatting | bytes 8192 | tf_op jit(solution)/shard_map/broadcast_in_dim | solution.py:979
  2.5 1.3 %broadcast_in_dim.21.gain = bf16[1,2048]{1,0:T(2,128)(2,1)} reshape(bf16[2048]{0:T(1024)(128)(2,1)} %param.18) | data formatting | bytes 8192 | tf_op jit(solution)/shard_map/broadcast_in_dim | solution.py:980
  3.7 1.4 %copy.15.page_owner = s32[128,1]{1,0:T(8,128)} copy(s32[128,1]{0,1:T(1,128)} %param.21) | data formatting | bytes 1024 | tf_op args[8]
  5.1 109.8 %prefill_pages.1 = (bf16[4096,512]{1,0:T(8,128)(2,1)}, bf16[128,2048]{1,0:T(8,128)(2,1)}, bf16[4,128,512]{2,1,0:T(8,128)(2,1)}, f32[4,8,128]{2,1,0:T(8,128)}) custom-call(bf16[2048,2048]{1,0:T(8,128)(2,1)} %embeds.1, bf16[128,7296]{1,0:T(8,128)(2,1)} %image_feats.1, bf16[1824,2048]{1,0:T(8,128)(2,1)} %proj_w.1, bf16[2048,2048]{1,0:T(8,128)(2,1)} %kv_w.1, ...), custom_call_target="tpu_custom_call" | custom-call | tf_op jit(solution)/shard_map/prefill_pages/pallas_call | solution.py:792
  114.9 0.0 copy-start
  114.9 6.4 %place_images.1 = bf16[4096,512]{1,0:T(8,128)(2,1)} custom-call(s32[4]{0:T(128)} %get-tuple-element.10.index_ref, s32[4]{0:T(128)} %get-tuple-element.11.offset_ref, bf16[4096,512]{1,0:T(8,128)(2,1)} %get-tuple-element.6.text, bf16[4,128,512]{2,1,0:T(8,128)(2,1)} %get-tuple-element.7.img, f32[4,8,128]{2,1,0:T(8,128)} %get-tuple-element.8.dest), custom_call_target="tpu_custom_call" | custom-call | tf_op jit(solution)/shard_map/place_images/pallas_call | solution.py:929
  121.3 0.0 copy-done
  121.3 0.8 copy.17
Async XLA Ops:
  114.9 6.4 %copy-start = (bf16[128,2048]{1,0:T(8,128)(2,1)S(1)}, bf16[128,2048]{1,0:T(8,128)(2,1)}, u32[]{:S(2)}) copy-start(bf16[128,2048]{1,0:T(8,128)(2,1)} %get-tuple-element.15) | copy-start | bytes 1572868

commit v2 on v1

--- a/solution.py
+++ b/solution.py
@@ -9,7 +9,7 @@
 
 HEAD = 128
 LANES = 128
-TILE = 512
+TILE = 256
 CORES = 2
 MESH = pl.DeviceIdType.MESH
 F32 = jnp.float32
@@ -18,6 +18,16 @@
 
 def ds(index, size):
     return pl.ds(pl.multiple_of(index * size, size), size)
+
+
+def flip(index, distance):
+    result = index
+    bit = 1
+    while bit <= distance:
+        if distance & bit:
+            result = result + bit - 2 * bit * lax.rem(index // bit, 2)
+        bit *= 2
+    return result
 
 
 def spread_rows(row):
@@ -46,6 +56,8 @@
     states_out,
     img_out,
     dest_out,
+    gain_rows,
+    bias_rows,
     sel,
     mask,
     dest,
@@ -145,10 +157,13 @@
     core = m % CORES
     partner = chip * CORES + (1 - core)
     peer = 1 - g
-    chunks, feat_local, _ = w_buf.shape
+    blocks, feat_local, _ = w_buf.shape
+    chunks = blocks // groups
     tokens = e_buf.shape[0]
     tiles = tokens // TILE
     steps = chunks * tiles
+    col_tile = min(512, feat_local)
+    col_tiles = feat_local // col_tile
     rows_img = hid.shape[0]
     half_rows = rows_img // groups
     core_rows = half_rows // CORES
@@ -175,9 +190,6 @@
     def seq_at(k):
         return lax.rem(s + k, seqs)
 
-    def seq_from(k):
-        return lax.rem(s + seqs - k, seqs)
-
     def mp_at(k):
         return lax.rem(m + k, mps)
 
@@ -187,9 +199,15 @@
     def e_copy(i):
         return pltpu.make_async_copy(embeds.at[ds(i, TILE), :], e_buf.at[ds(i, TILE), :], e_sem.at[i])
 
+    def half_at(b):
+        return lax.rem(g + b // chunks, groups)
+
+    def columns(b):
+        return half_at(b) * cols + b % chunks * LANES
+
     def w_copy(c, q, k):
         target = lax.rem(chip + k, chips) * CORES + (core if q == 0 else 1 - core)
-        start = target * block_cols + g * cols + c * LANES
+        start = target * block_cols + columns(c)
         return pltpu.make_async_copy(
             kv_w.at[:, pl.ds(pl.multiple_of(start, LANES), LANES)],
             w_buf.at[c, :, (q * chips + k) * LANES : (q * chips + k + 1) * LANES],
@@ -210,17 +228,27 @@
             w_copy(0, q, k).start()
     for i in range(1, tiles):
         e_copy(i).start()
-    for c in range(1, chunks):
-        for q in range(CORES):
-            for k in range(chips):
-                w_copy(c, q, k).start()
+    cache_first = pltpu.make_async_copy(
+        kv_cache.at[pl.ds(0, LANES // (queries.shape[1] // HEAD))], cache.at[0], cache_sem.at[0]
+    )
     pw_copy = pltpu.make_async_copy(proj_w, pw_buf, pw_sem)
-    pw_copy.start()
+
+    def later_loads():
+        pw_copy.start()
+        for c in range(1, blocks):
+            for q in range(CORES):
+                for k in range(chips):
+                    w_copy(c, q, k).start()
+
+        @pl.when(g != 0)
+        def _():
+            cache_first.start()
+
 
     f_load.wait()
     for b in range(seqs):
         feats[b] = f_rows[:, b * channels : (b + 1) * channels]
-    own_feats = pltpu.make_async_copy(feats.at[s], f_buf.at[s], fl_sem)
+    own_feats = pltpu.make_async_copy(feats.at[s], f_buf.at[0], fl_sem)
     own_feats.start()
 
     pl.semaphore_wait(barrier, seqs - 1 + mps - 1 + 1)
@@ -228,19 +256,18 @@
     def f_send(k):
         rows = ds(core, core_rows)
         return remote(
-            feats.at[seq_at(k), rows, :],
-            f_buf.at[s, rows, :],
+            feats.at[flip(s, k), rows, :],
+            f_buf.at[k, rows, :],
             send_f.at[k - 1],
             recv_f.at[k - 1],
-            seq=seq_at(k),
+            seq=flip(s, k),
         )
 
     def f_share(k):
         rows = ds(core, core_rows)
-        src = seq_from(k)
         return remote(
-            f_buf.at[src, rows, :],
-            f_buf.at[src, rows, :],
+            f_buf.at[k, rows, :],
+            f_buf.at[k, rows, :],
             send_fc.at[k - 1],
             recv_fc.at[k - 1],
             mp=partner,
@@ -251,6 +278,12 @@
 
     for k in range(1, seqs):
         f_send(k).start()
+
+    gain_rows[...] = gain[...].astype(F32)
+    biases = bias[...].astype(F32)
+    for j in range(feat_local // LANES):
+        t, within = divmod(j, col_tile // LANES)
+        bias_rows[t : t + 1, within * LANES : (within + 1) * LANES] = biases[j : j + 1, :]
 
     prompt = (s * tokens) // prompt_len
     limit = prompt_lengths[prompt]
@@ -258,8 +291,8 @@
     spots = image_pos[...] - s * tokens
     down = lax.broadcasted_iota(jnp.int32, (pages, LANES), 0)
     across = lax.broadcasted_iota(jnp.int32, (pages, LANES), 1)
-    owner_down = jnp.broadcast_to(page_owner[...].astype(F32), (pages, LANES))
-    owner_across = jnp.transpose(owner_down)
+    owner_across = jnp.broadcast_to(page_owner[...].astype(F32), (pages, LANES))
+    owner_down = jnp.transpose(owner_across)
     rank = jnp.sum(
         jnp.where((owner_down == owner_across) & (down < across), 1.0, 0.0), axis=0, keepdims=True
     )
@@ -301,9 +334,30 @@
     def sq_send(k):
         return remote(sq_own, sq_recv.at[k - 1], send_sq.at[k - 1], recv_sq.at[k - 1], mp=mp_at(k))
 
-    def p_copy(k):
+    far_first = range(seqs - 1, 0, -1)
+
+    levels = seqs.bit_length() - 1
+
+    def sent_at(level):
+        step_size = 2 << level
+        return list(range(1 << level, seqs, step_size))
+
+    def kept_at(level):
+        step_size = 2 << level
+        return list(range(0, seqs, step_size))
+
+    def base_at(level):
+        return seqs - (seqs >> level)
+
+    def p_copy(level, t):
+        span = pl.ds(base_at(level), len(sent_at(level)))
+        at = ds(t, col_tile)
         return remote(
-            p_send.at[seq_at(k)], p_recv.at[k - 1], send_r.at[k - 1], recv_r.at[k - 1], seq=seq_at(k)
+            p_send.at[span, :, at],
+            p_recv.at[span, :, at],
+            send_r.at[level, t],
+            recv_r.at[level, t],
+            seq=flip(s, 1 << level),
         )
 
     def scale_tile(i):
@@ -316,101 +370,96 @@
                 at = slice(j * LANES, (j + 1) * LANES)
                 value = e_buf[rows, at].astype(F32)
                 total = total + value * value
-                e_buf[rows, at] = (value * gain[:, at].astype(F32)).astype(BF16)
+                e_buf[rows, at] = (value * gain_rows[j : j + 1, :]).astype(BF16)
             sq_own[pl.ds(i * (TILE // LANES) + b, 1), :] = jnp.sum(
                 jnp.transpose(total), axis=0, keepdims=True
             )
             return carry
 
         lax.fori_loop(0, TILE // LANES, body, 0)
-
-    col_tile = min(512, feat_local)
 
     def project():
         for k in range(1, seqs):
             f_share(k).wait()
         own_feats.wait()
         pw_copy.wait()
-        spread = f_buf[...].reshape(seqs * half_rows, f_buf.shape[2])
+        spread = f_buf[...].reshape(seqs * half_rows, channels)
 
         def body(t, carry):
             at = ds(t, col_tile)
             out = jnp.dot(spread, pw_buf[:, at], preferred_element_type=F32)
             out = out.reshape(seqs, half_rows, col_tile)
-            p_send[:, :, at] = out.astype(BF16)
-            p_own[:, :, at] = out
-            for k in range(1, seqs):
-                remote(
-                    p_send.at[seq_at(k), :, at],
-                    p_recv.at[k - 1, :, at],
-                    send_r.at[k - 1],
-                    recv_r.at[k - 1],
-                    seq=seq_at(k),
-                ).start()
+            for slot_at, e in enumerate(sent_at(0)):
+                p_send[slot_at, :, at] = out[e].astype(BF16)
+            p_copy(0, t).start()
+            for slot_at, e in enumerate(kept_at(0)):
+                p_own[slot_at, :, at] = out[e]
             return carry
 
-        lax.fori_loop(0, feat_local // col_tile, body, 0)
-
-    share_step = min(tiles + 1, steps)
-    proj_step = min(tiles + 3, steps)
-
-    def step(n, carry):
-        @pl.when(n < steps)
-        def _():
-            c, i = n // tiles, lax.rem(n, tiles)
-
-            @pl.when(n == 0)
+        lax.fori_loop(0, col_tiles, body, 0)
+
+    def reduce_level(level):
+        def body(t, carry):
+            at = ds(t, col_tile)
+            p_copy(level, t).wait()
+            for index in range(len(kept_at(level))):
+                total = p_own[index, :, at] + p_recv[base_at(level) + index, :, at].astype(F32)
+                if index % 2 == 0:
+                    p_own[index // 2, :, at] = total
+                else:
+                    p_send[base_at(level + 1) + index // 2, :, at] = total.astype(BF16)
+            p_copy(level + 1, t).start()
+            return carry
+
+        lax.fori_loop(0, col_tiles, body, 0)
+
+    def combine(p):
+        c, i = p // tiles, lax.rem(p, tiles)
+        first(p).wait()
+        total = acc1[lax.rem(p, 2)] + r1[p].astype(F32)
+        acc2[c, ds(i, TILE), :] = total[:, :LANES]
+        for k in range(1, chips):
+            s2[p, k - 1] = total[:, k * LANES : (k + 1) * LANES].astype(BF16)
+            second(p, k).start()
+
+    def multiply(n, c, i):
+        part = jnp.dot(e_buf[ds(i, TILE), :], w_buf[c], preferred_element_type=F32)
+        acc1[lax.rem(n, 2)] = part[:, :own_cols]
+        s1[n] = part[:, own_cols:].astype(BF16)
+        first(n).start()
+
+    def text_chunk(c):
+        for q in range(CORES):
+            for k in range(chips):
+                w_copy(c, q, k).wait()
+
+        def body(i, carry):
+            if c == 0:
+                scale_tile(i)
+
+                @pl.when(i == tiles // 2)
+                def _():
+                    later_loads()
+
+            multiply(c * tiles + i, c, i)
+
+            @pl.when(i > 0)
             def _():
-                for q in range(CORES):
-                    for k in range(chips):
-                        w_copy(0, q, k).wait()
-
-            for cc in range(1, chunks):
-
-                @pl.when(n == cc * tiles)
-                def _():
-                    for q in range(CORES):
-                        for k in range(chips):
-                            w_copy(cc, q, k).wait()
-
-            @pl.when(c == 0)
-            def _():
-                scale_tile(i)
-
-            part = jnp.dot(e_buf[ds(i, TILE), :], w_buf[c], preferred_element_type=F32)
-            acc1[lax.rem(n, 2)] = part[:, :own_cols]
-            s1[n] = part[:, own_cols:].astype(BF16)
-            first(n).start()
-
-            @pl.when(n == tiles - 1)
-            def _():
-                for k in range(1, mps):
-                    sq_send(k).start()
-
-        @pl.when(n == share_step)
-        def _():
-            for k in range(1, seqs):
-                f_send(k).wait_recv()
-                f_share(k).start()
-
-        @pl.when(n > 0)
-        def _():
-            p = n - 1
-            c, i = p // tiles, lax.rem(p, tiles)
-            first(p).wait()
-            total = acc1[lax.rem(p, 2)] + r1[p].astype(F32)
-            acc2[c, ds(i, TILE), :] = total[:, :LANES]
-            for k in range(1, chips):
-                s2[p, k - 1] = total[:, k * LANES : (k + 1) * LANES].astype(BF16)
-                second(p, k).start()
-
-        @pl.when(n == proj_step)
-        def _():
-            project()
-
-        return carry
-
-    lax.fori_loop(0, steps + 1, step, 0)
+                combine(c * tiles + i - 1)
+
+            return carry
+
+        lax.fori_loop(0, tiles, body, 0)
+        if c == 0:
+            for k in range(1, mps):
+                sq_send(k).start()
+        combine(c * tiles + tiles - 1)
+
+    text_chunk(0)
+    for k in range(1, seqs):
+        f_send(k).wait_recv()
+        f_share(k).start()
+    project()
 
     for k in range(1, mps):
         sq_send(k).wait()
@@ -421,11 +470,11 @@
 
     def z_send(c, k):
         return remote(
-            by_owner.at[c, ds(seq_at(k), block), :],
+            by_owner.at[c, ds(flip(s, k), block), :],
             arrived.at[c, ds(s, block), :],
             send_z.at[c, k - 1],
             recv_z.at[c, k - 1],
-            seq=seq_at(k),
+            seq=flip(s, k),
         )
 
     def out_at(rows, half, c):
@@ -458,26 +507,25 @@
         )
 
     def finish(c):
-        for i in range(tiles):
+        def body(i, carry):
+            n = c * tiles + i
             for k in range(1, chips):
-                second(c * tiles + i, k).wait()
-
-        def body(b, carry):
-            rows = ds(b, LANES)
-            n = c * tiles + b // (TILE // LANES)
-            within = ds(lax.rem(b, TILE // LANES), LANES)
-            value = acc2[c, rows, :]
-            for k in range(1, chips):
-                value = value + r2[n, k - 1, within, :].astype(F32)
-            value = value * spread_rows(scale[pl.ds(b, 1), :])
-            acc2[c, rows, :] = value
-            kv_send[c, rows, :] = value.astype(BF16)
+                second(n, k).wait()
+            for b in range(TILE // LANES):
+                rows = pl.ds(pl.multiple_of(i * TILE + b * LANES, LANES), LANES)
+                within = pl.ds(b * LANES, LANES)
+                value = acc2[c, rows, :]
+                for k in range(1, chips):
+                    value = value + r2[n, k - 1, within, :].astype(F32)
+                value = value * spread_rows(scale[pl.ds(i * (TILE // LANES) + b, 1), :])
+                acc2[c, rows, :] = value
+                kv_send[c, rows, :] = value.astype(BF16)
             return carry
 
-        lax.fori_loop(0, tokens // LANES, body, 0)
+        lax.fori_loop(0, tiles, body, 0)
         select(c, by_owner)
-        for k in range(1, seqs):
-            z_send(c, k).start()
+
+    def own_sends(c):
         mine = ds(s, block)
 
         @pl.when(g == 0)
@@ -487,6 +535,7 @@
 
         @pl.when(g != 0)
         def _():
+            k_send(c).start()
             local(by_owner.at[c, mine, :], mine, c).start()
 
     def take_peer(c):
@@ -497,7 +546,7 @@
 
     def forward(c, k):
         z_send(c, k).wait_recv()
-        rows = ds(seq_from(k), block)
+        rows = ds(flip(s, k), block)
 
         @pl.when(g == 0)
         def _():
@@ -506,116 +555,6 @@
         @pl.when(g != 0)
         def _():
             local(arrived.at[c, rows, :], rows, c).start()
-
-    finish(0)
-
-    for k in range(1, seqs):
-        p_copy(k).wait()
-    own_rows = ds(g, half_rows)
-
-    def gelu_body(t, carry):
-        at = ds(t, col_tile)
-        total = p_own[s, :, at] + bias[:, at].astype(F32)
-        for k in range(1, seqs):
-            total = total + p_recv[k - 1, :, at].astype(F32)
-        hid[own_rows, at] = (
-            0.5 * total * (1.0 + lax.erf(total * 0.5**0.5))
-        ).astype(BF16)
-        return carry
-
-    lax.fori_loop(0, feat_local // col_tile, gelu_body, 0)
-    h_send = remote(hid.at[own_rows, :], hid.at[own_rows, :], send_h, recv_h, group=peer)
-    h_send.start()
-
-
-    @pl.when(g != 0)
-    def _():
-        k_send(0).start()
-
-    for c in range(1, chunks):
-        finish(c)
-    forward(0, 1)
-
-    h_send.wait()
-
-    @pl.when(g != 0)
-    def _():
-        for c in range(1, chunks):
-            k_send(c).start()
-
-    hid_copy = pltpu.make_async_copy(hid, states_out, misc_sem.at[1])
-
-    @pl.when(g == 0)
-    def _():
-        hid_copy.start()
-
-    total = jnp.zeros((rows_img, LANES), F32)
-    for j in range(feat_local // LANES):
-        at = slice(j * LANES, (j + 1) * LANES)
-        value = hid[:, at].astype(F32)
-        total = total + value * value
-        i_scaled[:, at] = (value * gain[:, at].astype(F32)).astype(BF16)
-    isq_own[...] = jnp.broadcast_to(
-        jnp.sum(jnp.transpose(total), axis=0, keepdims=True), isq_own.shape
-    )
-
-    def iq_send(k):
-        return remote(isq_own, isq_recv.at[k - 1], send_iq.at[k - 1], recv_iq.at[k - 1], mp=mp_at(k))
-
-    for k in range(1, mps):
-        iq_send(k).start()
-    for c in range(chunks):
-        part = jnp.dot(i_scaled[...], w_buf[c], preferred_element_type=F32)
-        i_acc[c] = part[:, :own_cols]
-        is1[c] = part[:, own_cols:].astype(BF16)
-    i_first = remote(is1, ir1, send_i1, recv_i1, mp=partner)
-    i_first.start()
-
-    def i_second(k):
-        return remote(
-            is2.at[k - 1], ir2.at[k - 1], send_i2.at[k - 1], recv_i2.at[k - 1], mp=chip_at(k)
-        )
-
-    i_first.wait()
-    for c in range(chunks):
-        total = i_acc[c] + ir1[c].astype(F32)
-        i_acc[c] = total
-        for k in range(1, chips):
-            is2[k - 1, c] = total[:, k * LANES : (k + 1) * LANES].astype(BF16)
-    for k in range(1, chips):
-        i_second(k).start()
-    for k in range(1, mps):
-        iq_send(k).wait()
-    squares = isq_own[...]
-    for k in range(1, mps):
-        squares = squares + isq_recv[k - 1]
-    i_scale = spread_rows(lax.rsqrt(squares / width + 1e-05)[:1])
-    for k in range(1, chips):
-        i_second(k).wait()
-    for c in range(chunks):
-        value = i_acc[c, :, :LANES]
-        for k in range(1, chips):
-            value = value + ir2[k - 1, c].astype(F32)
-        ikv[:, c * LANES : (c + 1) * LANES] = (value * i_scale).astype(BF16)
-
-    def img_at(index, half):
-        return img_out.at[index, :, pl.ds(pl.multiple_of(half * cols, cols), cols)]
-
-    def iz_send(k):
-        return remote(ikv, img_at(s, g), send_iz.at[k - 1], recv_iz.at[k - 1], seq=seq_at(k))
-
-    iy_send = remote(ikv, img_at(s, g), send_iy, recv_iy, group=peer)
-    for k in range(1, seqs):
-        iz_send(k).start()
-    iy_send.start()
-    i_local = pltpu.make_async_copy(ikv, img_at(s, g), misc_sem.at[2])
-    i_local.start()
-
-    def if_send(k):
-        src = seq_from(k)
-        return remote(
-            img_at(src, 0), img_at(src, 0), send_if.at[k - 1], recv_if.at[k - 1], group=peer
-        )
 
     heads = queries.shape[1] // HEAD
     kv_heads = kv_cache.shape[2] // (2 * HEAD)
@@ -683,39 +622,173 @@
 
     att_copy = pltpu.make_async_copy(attended, states_out, misc_sem.at[1])
 
-    @pl.when(g != 0)
-    def _():
-        cache_copy(0).start()
+    batches = rows_dec // batch
+
+    def attend_start():
         for j in range(heads):
             q_rows[pl.ds(j, rows_dec, stride=heads), :] = queries[
                 :, j * HEAD : (j + 1) * HEAD
             ].astype(F32)
         fresh[...] = new_kv[...].astype(F32)
         lengths[...] = spread_rows(cache_lengths[...].astype(F32))
-        lax.fori_loop(0, rows_dec // batch, attend_batch, 0)
-        for j in range(heads):
-            attended[:, j * HEAD : (j + 1) * HEAD] = a_rows[
-                pl.ds(j, rows_dec, stride=heads), :
-            ].astype(BF16)
-        att_copy.start()
-
-    for k in range(2, seqs):
-        forward(0, k)
+
+    def attend(low, high):
+        @pl.when(g != 0)
+        def _():
+            if low == 0:
+                attend_start()
+            lax.fori_loop(low, high, attend_batch, 0)
+            if high == batches:
+                for j in range(heads):
+                    attended[:, j * HEAD : (j + 1) * HEAD] = a_rows[
+                        pl.ds(j, rows_dec, stride=heads), :
+                    ].astype(BF16)
+                att_copy.start()
+
+    finish(0)
+    z_send(0, 1).start()
+    for k in far_first:
+        if k not in (1, seqs // 2):
+            z_send(0, k).start()
+    own_sends(0)
+    for c in range(1, chunks):
+        text_chunk(c)
+    for level in range(levels - 1):
+        reduce_level(level)
+    z_send(0, seqs // 2).start()
+    forward(0, 1)
+    for c in range(1, chunks):
+        finish(c)
+        z_send(c, 1).start()
+        own_sends(c)
+    forward(0, seqs - 1)
+
+    own_rows = ds(g, half_rows)
+
+    def gelu_body(t, carry):
+        at = ds(t, col_tile)
+        p_copy(levels - 1, t).wait()
+        total = p_own[0, :, at] + p_recv[base_at(levels - 1), :, at].astype(F32)
+        total = total + bias_rows[pl.ds(t, 1), :]
+        hid[own_rows, at] = (0.5 * total * (1.0 + lax.erf(total * 0.5**0.5))).astype(BF16)
+        return carry
+
+    lax.fori_loop(0, col_tiles, gelu_body, 0)
+    h_send = remote(hid.at[own_rows, :], hid.at[own_rows, :], send_h, recv_h, group=peer)
+
+    @pl.when(g != 0)
+    def _():
+        h_send.start()
+
+    for c in range(1, chunks):
+        for k in far_first:
+            if k not in (1, seqs // 2):
+                z_send(c, k).start()
+        forward(c, 1)
+
+    total = jnp.zeros((half_rows, LANES), F32)
+    for j in range(feat_local // LANES):
+        at = slice(j * LANES, (j + 1) * LANES)
+        value = hid[own_rows, at].astype(F32)
+        total = total + value * value
+        i_scaled[:, at] = (value * gain_rows[j : j + 1, :]).astype(BF16)
+    total = jnp.concatenate([total, jnp.zeros((LANES - half_rows, LANES), F32)], axis=0)
+    isq_own[...] = jnp.broadcast_to(
+        jnp.sum(jnp.transpose(total), axis=0, keepdims=True), isq_own.shape
+    )
+
+    def iq_send(k):
+        return remote(isq_own, isq_recv.at[k - 1], send_iq.at[k - 1], recv_iq.at[k - 1], mp=mp_at(k))
+
+    for k in range(1, mps):
+        iq_send(k).start()
+    for c in range(chunks, blocks):
+        for q in range(CORES):
+            for k in range(chips):
+                w_copy(c, q, k).wait()
+    for b in range(blocks):
+        part = jnp.dot(i_scaled[...], w_buf[b], preferred_element_type=F32)
+        i_acc[b] = part[:, :own_cols]
+        is1[b] = part[:, own_cols:].astype(BF16)
+    i_first = remote(is1, ir1, send_i1, recv_i1, mp=partner)
+    i_first.start()
+
+    def i_second(k):
+        return remote(
+            is2.at[k - 1], ir2.at[k - 1], send_i2.at[k - 1], recv_i2.at[k - 1], mp=chip_at(k)
+        )
+
+    i_first.wait()
+    for b in range(blocks):
+        total = i_acc[b] + ir1[b].astype(F32)
+        i_acc[b] = total
+        for k in range(1, chips):
+            is2[k - 1, b] = total[:, k * LANES : (k + 1) * LANES].astype(BF16)
+    for k in range(1, chips):
+        i_second(k).start()
+    for k in range(1, mps):
+        iq_send(k).wait()
+    squares = isq_own[...]
+    for k in range(1, mps):
+        squares = squares + isq_recv[k - 1]
+    i_scale = spread_rows(lax.rsqrt(squares / width + 1e-05)[:1])[:half_rows]
+    for k in range(1, chips):
+        i_second(k).wait()
+    for b in range(blocks):
+        value = i_acc[b, :, :LANES]
+        for k in range(1, chips):
+            value = value + ir2[k - 1, b].astype(F32)
+        ikv[:, pl.ds(pl.multiple_of(columns(b), LANES), LANES)] = (value * i_scale).astype(BF16)
+
+    def img_at(index, half):
+        return img_out.at[index, ds(half, half_rows), :]
+
+    def iz_send(k):
+        return remote(ikv, img_at(s, g), send_iz.at[k - 1], recv_iz.at[k - 1], seq=flip(s, k))
+
+    iy_send = remote(ikv, img_at(s, g), send_iy, recv_iy, group=peer)
+    for k in far_first:
+        iz_send(k).start()
+    iy_send.start()
+    i_local = pltpu.make_async_copy(ikv, img_at(s, g), misc_sem.at[2])
+    i_local.start()
+    for c in range(1, chunks):
+        z_send(c, seqs // 2).start()
+    attend(0, batches)
+    for k in far_first:
+        if k not in (1, seqs - 1):
+            forward(0, k)
+
+    def if_send(k):
+        src = flip(s, k)
+        return remote(
+            img_at(src, 0), img_at(src, 0), send_if.at[k - 1], recv_if.at[k - 1], group=peer
+        )
+
 
     @pl.when(g == 0)
     def _():
         for c in range(chunks):
             take_peer(c)
 
-    for c in range(1, chunks):
-        for k in range(1, seqs):
-            forward(c, k)
-    for k in range(1, seqs):
+    for k in far_first:
         iz_send(k).wait_recv()
 
         @pl.when(g == 0)
         def _():
             if_send(k).start()
+
+    hid_copy = pltpu.make_async_copy(hid, states_out, misc_sem.at[1])
+
+    @pl.when(g == 0)
+    def _():
+        h_send.wait_recv()
+        hid_copy.start()
+
+    for c in range(1, chunks):
+        for k in far_first:
+            if k != 1:
+                forward(c, k)
 
     for c in range(chunks):
         for k in range(1, seqs):
@@ -744,6 +817,10 @@
         @pl.when(g != 0)
         def _():
             if_send(k).wait_recv()
+
+    @pl.when(g != 0)
+    def _():
+        h_send.wait_send()
 
     iy_send.wait()
     i_local.wait()
@@ -778,8 +855,12 @@
     block_cols = kv_w.shape[1] // mps
     cols = block_cols // groups
     chunks = cols // LANES
+    blocks = groups * chunks
     steps = chunks * tiles
-    pages = page_owner.shape[0]
+    col_tile = min(512, feat_local)
+    col_tiles = feat_local // col_tile
+    levels = seqs.bit_length() - 1
+    pages = page_owner.shape[1]
     page = tokens // pages
     slots = seqs * (2 * pages // seqs)
     rows_dec = queries.shape[0]
@@ -800,13 +881,15 @@
         in_specs=[anywhere] * 5 + [vmem] * 7 + [pl.BlockSpec(memory_space=pltpu.SMEM)],
         out_specs=(anywhere,) * 4,
         scratch_shapes=[
+            pltpu.VMEM((feat_local // LANES, LANES), F32),
+            pltpu.VMEM((col_tiles, col_tile), F32),
             pltpu.VMEM((slots, pages), BF16),
             pltpu.VMEM((dense, LANES), F32),
             pltpu.VMEM((8, rows_img), F32),
             pltpu.VMEM((half_rows, all_channels), BF16),
             pltpu.VMEM((seqs, half_rows, channels), BF16),
             pltpu.VMEM((tokens, feat_local), BF16),
-            pltpu.VMEM((chunks, feat_local, mps * LANES), BF16),
+            pltpu.VMEM((blocks, feat_local, mps * LANES), BF16),
             pltpu.VMEM((channels, feat_local), BF16),
             pltpu.VMEM((seqs, half_rows, channels), BF16),
             pltpu.VMEM((2, TILE, chips * LANES), F32),
@@ -824,19 +907,19 @@
             pltpu.VMEM((chunks, tokens, LANES), BF16),
             pltpu.VMEM((chunks, tokens, LANES), BF16),
             pltpu.VMEM((chunks, slots * page, LANES), BF16),
-            pltpu.VMEM((seqs, half_rows, feat_local), F32),
-            pltpu.VMEM((seqs, half_rows, feat_local), BF16),
+            pltpu.VMEM((seqs // 2, half_rows, feat_local), F32),
+            pltpu.VMEM((seqs - 1, half_rows, feat_local), BF16),
             pltpu.VMEM((seqs - 1, half_rows, feat_local), BF16),
             pltpu.VMEM((rows_img, feat_local), BF16),
-            pltpu.VMEM((rows_img, feat_local), BF16),
-            pltpu.VMEM((chunks, rows_img, chips * LANES), F32),
-            pltpu.VMEM((chunks, rows_img, chips * LANES), BF16),
-            pltpu.VMEM((chunks, rows_img, chips * LANES), BF16),
-            pltpu.VMEM((chips - 1, chunks, rows_img, LANES), BF16),
-            pltpu.VMEM((chips - 1, chunks, rows_img, LANES), BF16),
+            pltpu.VMEM((half_rows, feat_local), BF16),
+            pltpu.VMEM((blocks, half_rows, chips * LANES), F32),
+            pltpu.VMEM((blocks, half_rows, chips * LANES), BF16),
+            pltpu.VMEM((blocks, half_rows, chips * LANES), BF16),
+            pltpu.VMEM((chips - 1, blocks, half_rows, LANES), BF16),
+            pltpu.VMEM((chips - 1, blocks, half_rows, LANES), BF16),
             pltpu.VMEM((8, LANES), F32),
             pltpu.VMEM((mps - 1, 8, LANES), F32),
-            pltpu.VMEM((rows_img, cols), BF16),
+            pltpu.VMEM((half_rows, block_cols), BF16),
             pltpu.VMEM((rows_dec * heads, HEAD), F32),
             pltpu.VMEM(new_kv.shape, F32),
             pltpu.VMEM((rows_dec, LANES), F32),
@@ -849,7 +932,7 @@
             pltpu.VMEM(queries.shape, BF16),
             dma((1,)),
             dma((2,)),
-            dma((chunks, mps)),
+            dma((blocks, mps)),
             dma((tiles,)),
             dma,
             dma,
@@ -863,8 +946,8 @@
             dma((seqs - 1,)),
             dma((seqs - 1,)),
             dma((seqs - 1,)),
-            dma((seqs - 1,)),
-            dma((seqs - 1,)),
+            dma((levels, col_tiles)),
+            dma((levels, col_tiles)),
             dma,
             dma,
             dma,
@@ -912,35 +995,61 @@
     )
 
 
-def patch_kernel(index_ref, offset_ref, text, img, dest, out):
-    rows = text.shape[0]
-    first = offset_ref[pl.program_id(0)]
-    spots = (dest[0, :1, :] - first.astype(F32)).astype(jnp.int32)
-    hit = lax.broadcasted_iota(jnp.int32, (rows, dest.shape[2]), 0) == spots
-    placed = jnp.dot(
-        jnp.where(hit, 1.0, 0.0).astype(BF16), img[0], preferred_element_type=F32
-    )
-    out[...] = (text[...].astype(F32) + placed).astype(BF16)
-
-
-def patch(index, offset, text, img, dest):
-    seqs, rows_img, block_cols = img.shape
-    block = text.shape[0] // seqs
+def place_kernel(index, offset, text, img, dest, states, out, states_out, rows, state_rows, sems):
+    parts = index.shape[0]
+    block = text.shape[0] // parts
+
+    def load(b):
+        span = pl.ds(b * block, block)
+        return pltpu.make_async_copy(text.at[span, :], rows.at[span, :], sems.at[0, b])
+
+    def store(b):
+        span = pl.ds(b * block, block)
+        return pltpu.make_async_copy(rows.at[span, :], out.at[span, :], sems.at[1, b])
+
+    state_load = pltpu.make_async_copy(states, state_rows, sems.at[2, 0])
+    state_store = pltpu.make_async_copy(state_rows, states_out, sems.at[2, 1])
+    for b in range(parts):
+        load(b).start()
+    state_load.start()
+    for b in range(parts):
+        spots = dest[index[b]][:1].astype(jnp.int32) - offset[b]
+        hit = lax.broadcasted_iota(jnp.int32, (block, dest.shape[2]), 0) == spots
+        placed = jnp.dot(
+            jnp.where(hit, 1.0, 0.0).astype(BF16), img[index[b]], preferred_element_type=F32
+        )
+        load(b).wait()
+        span = pl.ds(b * block, block)
+        rows[span, :] = rows[span, :] + placed.astype(BF16)
+        store(b).start()
+        if b == 0:
+            state_load.wait()
+            state_store.start()
+    for b in range(parts):
+        store(b).wait()
+    state_store.wait()
+
+
+def place(index, offset, text, img, dest, states):
+    parts = index.shape[0]
+    smem = pl.BlockSpec(memory_space=pltpu.SMEM)
+    vmem = pl.BlockSpec(memory_space=pltpu.VMEM)
+    anywhere = pl.BlockSpec(memory_space=pl.ANY)
     return pl.pallas_call(
-        patch_kernel,
-        out_shape=jax.ShapeDtypeStruct(text.shape, text.dtype),
-        grid_spec=pltpu.PrefetchScalarGridSpec(
-            num_scalar_prefetch=2,
-            grid=(seqs,),
-            in_specs=[
-                pl.BlockSpec((block, block_cols), lambda b, index, offset: (b, 0)),
-                pl.BlockSpec((1, rows_img, block_cols), lambda b, index, offset: (index[b], 0, 0)),
-                pl.BlockSpec((1, 8, rows_img), lambda b, index, offset: (index[b], 0, 0)),
-            ],
-            out_specs=pl.BlockSpec((block, block_cols), lambda b, index, offset: (b, 0)),
+        place_kernel,
+        out_shape=(
+            jax.ShapeDtypeStruct(text.shape, text.dtype),
+            jax.ShapeDtypeStruct(states.shape, states.dtype),
         ),
+        in_specs=[smem, smem, anywhere, vmem, vmem, anywhere],
+        out_specs=(anywhere, anywhere),
+        scratch_shapes=[
+            pltpu.VMEM(text.shape, text.dtype),
+            pltpu.VMEM(states.shape, states.dtype),
+            pltpu.SemaphoreType.DMA((3, max(parts, 2))),
+        ],
         name="place_images",
-    )(index, offset, text, img, dest)
+    )(index, offset, text, img, dest, states)
 
 
 def per_device(
@@ -976,18 +1085,21 @@
         kv_w,
         kv_cache,
         image_pos[None, :],
-        proj_b[None, :],
-        norm_gain[None, :],
-        page_owner,
+        proj_b.reshape(-1, LANES),
+        norm_gain.reshape(-1, LANES),
+        page_owner.reshape(1, -1),
         queries,
         new_kv,
         cache_lengths[None, :],
         prompt_lengths,
     )
-    order = jnp.arange(seqs, dtype=jnp.int32)
-    index = jnp.where(prefill_side, seq_index, order)
-    offset = jnp.where(prefill_side, order, seq_index) * (capacity * page)
-    page_slots = patch(index, offset, text, img, dest_all)
+    parts = max(1, 8 // seqs)
+    order = jnp.arange(seqs * parts, dtype=jnp.int32)
+    source, part = order // parts, order % parts
+    index = jnp.where(prefill_side, seq_index, source)
+    offset = jnp.where(prefill_side, source, seq_index) * (capacity * page)
+    offset = offset + part * (capacity * page // parts)
+    page_slots, row_states = place(index, offset, text, img, dest_all, row_states)
     page_slots = page_slots.reshape(-1, page, text.shape[1])
     return (page_slots, row_states)
 

time: 124 us -> 112 us (0.903)
  Pallas kernels: 116 us -> 110 us
  local copies, waits for them, and re-layouts: 4.76 us -> 0 us
    pallas_call x1, Pallas kernels: 110 us -> 103 us  [prefill(): pl.pallas_call(functools.partial(prefill_kernel, groups, seqs, mps, promp...]
    broadcast_in_dim x2 -> x0, local copies, waits for them, and re-layouts: 2.57 us -> none  [the longest x1 1.29 us: per_device(): proj_b[None, :]]
    unnamed x4 -> x0, local copies, waits for them, and re-layouts: 2.19 us -> none
where the time goes in v2:
time: 112 us; the launch traced here: 111 us
  Pallas kernels  110 us (98%)
    pallas_call x1, Pallas kernels, prefill(): pl.pallas_call(functools.partial(prefill_kernel, groups, seqs, mps, promp...  103 us
    pallas_call x1, Pallas kernels, place(): pl.pallas_call(place_kernel, out_shape=(jax.ShapeDtypeStruct(text.shape,...  6.87 us

profile of v2, /device:TPU:0, one launch (start us, length us, event | category | flops | bytes accessed | tf_op | source)
XLA Modules:
  0.0 111.0 jit_solution(4775406630287807543)
XLA Ops:
  0.6 0.5 broadcast_select_fusion.1
  1.2 102.9 %prefill_pages.1 = (bf16[4096,512]{1,0:T(8,128)(2,1)}, bf16[128,2048]{1,0:T(8,128)(2,1)}, bf16[4,128,512]{2,1,0:T(8,128)(2,1)}, f32[4,8,128]{2,1,0:T(8,128)}) custom-call(bf16[2048,2048]{1,0:T(8,128)(2,1)} %embeds.1, bf16[128,7296]{1,0:T(8,128)(2,1)} %image_feats.1, bf16[1824,2048]{1,0:T(8,128)(2,1)} %proj_w.1, bf16[2048,2048]{1,0:T(8,128)(2,1)} %kv_w.1, ...), custom_call_target="tpu_custom_call" | custom-call | tf_op jit(solution)/shard_map/prefill_pages/pallas_call | solution.py:873
  104.1 6.9 %place_images.1 = (bf16[4096,512]{1,0:T(8,128)(2,1)}, bf16[128,2048]{1,0:T(8,128)(2,1)}) custom-call(s32[8]{0:T(128)} %get-tuple-element.14.index, s32[8]{0:T(128)} %get-tuple-element.15.offset, bf16[4096,512]{1,0:T(8,128)(2,1)} %get-tuple-element.8.text, bf16[4,128,512]{2,1,0:T(8,128)(2,1)} %get-tuple-element.9.img, f32[4,8,128]{2,1,0:T(8,128)} %get-tuple-element.10.dest, ...), custom_call_target="tpu_custom_call" | custom-call | tf_op jit(solution)/shard_map/place_images/pallas_call | solution.py:1038

commit v3 on v2

--- a/solution.py
+++ b/solution.py
@@ -335,6 +335,7 @@
         return remote(sq_own, sq_recv.at[k - 1], send_sq.at[k - 1], recv_sq.at[k - 1], mp=mp_at(k))
 
     far_first = range(seqs - 1, 0, -1)
+    outer = lax.rem(s, 2) == lax.rem(s // 2, 2)
 
     levels = seqs.bit_length() - 1
 
@@ -468,14 +469,21 @@
         squares = squares + sq_recv[k - 1]
     scale[...] = mask[...] * lax.rsqrt(squares / width + 1e-05)
 
-    def z_send(c, k):
+    halves = 2
+    piece = block // halves
+
+    def z_piece(c, k, h):
         return remote(
-            by_owner.at[c, ds(flip(s, k), block), :],
-            arrived.at[c, ds(s, block), :],
-            send_z.at[c, k - 1],
-            recv_z.at[c, k - 1],
+            by_owner.at[c, ds(flip(s, k) * halves + h, piece), :],
+            arrived.at[c, ds(s * halves + h, piece), :],
+            send_z.at[c, (k - 1) * halves + h],
+            recv_z.at[c, (k - 1) * halves + h],
             seq=flip(s, k),
         )
+
+    def z_start(c, k):
+        for h in range(halves):
+            z_piece(c, k, h).start()
 
     def out_at(rows, half, c):
         at = pl.ds(pl.multiple_of(half * cols + c * LANES, LANES), LANES)
@@ -545,16 +553,17 @@
         local2(c).start()
 
     def forward(c, k):
-        z_send(c, k).wait_recv()
-        rows = ds(flip(s, k), block)
-
-        @pl.when(g == 0)
-        def _():
-            y_send(arrived.at[c, rows, :], rows, c).start()
-
-        @pl.when(g != 0)
-        def _():
-            local(arrived.at[c, rows, :], rows, c).start()
+        for h in range(halves):
+            z_piece(c, k, h).wait_recv()
+            rows = ds(flip(s, k) * halves + h, piece)
+
+            @pl.when(g == 0)
+            def _():
+                y_send(arrived.at[c, rows, :], rows, c).start()
+
+            @pl.when(g != 0)
+            def _():
+                local(arrived.at[c, rows, :], rows, c).start()
 
     heads = queries.shape[1] // HEAD
     kv_heads = kv_cache.shape[2] // (2 * HEAD)
@@ -646,21 +655,21 @@
                 att_copy.start()
 
     finish(0)
-    z_send(0, 1).start()
+    z_start(0, 1)
     for k in far_first:
         if k not in (1, seqs // 2):
-            z_send(0, k).start()
+            z_start(0, k)
     own_sends(0)
     for c in range(1, chunks):
         text_chunk(c)
     for level in range(levels - 1):
         reduce_level(level)
-    z_send(0, seqs // 2).start()
-    forward(0, 1)
+    z_start(0, seqs // 2)
     for c in range(1, chunks):
         finish(c)
-        z_send(c, 1).start()
+        z_start(c, 1)
         own_sends(c)
+    forward(0, 1)
     forward(0, seqs - 1)
 
     own_rows = ds(g, half_rows)
@@ -683,7 +692,7 @@
     for c in range(1, chunks):
         for k in far_first:
             if k not in (1, seqs // 2):
-                z_send(c, k).start()
+                z_start(c, k)
         forward(c, 1)
 
     total = jnp.zeros((half_rows, LANES), F32)
@@ -753,7 +762,7 @@
     i_local = pltpu.make_async_copy(ikv, img_at(s, g), misc_sem.at[2])
     i_local.start()
     for c in range(1, chunks):
-        z_send(c, seqs // 2).start()
+        z_start(c, seqs // 2)
     attend(0, batches)
     for k in far_first:
         if k not in (1, seqs - 1):
@@ -771,13 +780,6 @@
         for c in range(chunks):
             take_peer(c)
 
-    for k in far_first:
-        iz_send(k).wait_recv()
-
-        @pl.when(g == 0)
-        def _():
-            if_send(k).start()
-
     hid_copy = pltpu.make_async_copy(hid, states_out, misc_sem.at[1])
 
     @pl.when(g == 0)
@@ -785,14 +787,41 @@
         h_send.wait_recv()
         hid_copy.start()
 
+    rest = [k for k in far_first if k != 1]
     for c in range(1, chunks):
-        for k in far_first:
-            if k != 1:
+
+        @pl.when(outer)
+        def _():
+            forward(c, rest[0])
+
+        @pl.when(jnp.logical_not(outer))
+        def _():
+            forward(c, rest[-1])
+
+    for k in far_first:
+        iz_send(k).wait_recv()
+
+        @pl.when(g == 0)
+        def _():
+            if_send(k).start()
+
+    for c in range(1, chunks):
+
+        @pl.when(outer)
+        def _():
+            for k in rest[1:]:
                 forward(c, k)
+
+        @pl.when(jnp.logical_not(outer))
+        def _():
+            for k in rest[:-1]:
+                forward(c, k)
+
 
     for c in range(chunks):
         for k in range(1, seqs):
-            z_send(c, k).wait_send()
+            for h in range(halves):
+                z_piece(c, k, h).wait_send()
         local(by_owner.at[c], everything, c).wait()
 
         @pl.when(g == 0)
@@ -873,13 +902,13 @@
     return pl.pallas_call(
         functools.partial(prefill_kernel, groups, seqs, mps, prompt_len),
         out_shape=(
-            jax.ShapeDtypeStruct((slots * page, block_cols), BF16),
-            jax.ShapeDtypeStruct((rows_img, feat_local), BF16),
-            jax.ShapeDtypeStruct((seqs, rows_img, block_cols), BF16),
-            jax.ShapeDtypeStruct((seqs, 8, rows_img), F32),
+            pltpu.VMEM((slots * page, block_cols), BF16),
+            pltpu.VMEM((rows_img, feat_local), BF16),
+            pltpu.VMEM((seqs, rows_img, block_cols), BF16),
+            pltpu.VMEM((seqs, 8, rows_img), F32),
         ),
         in_specs=[anywhere] * 5 + [vmem] * 7 + [pl.BlockSpec(memory_space=pltpu.SMEM)],
-        out_specs=(anywhere,) * 4,
+        out_specs=(vmem,) * 4,
         scratch_shapes=[
             pltpu.VMEM((feat_local // LANES, LANES), F32),
             pltpu.VMEM((col_tiles, col_tile), F32),
@@ -956,8 +985,8 @@
             dma((chips - 1,)),
             dma((mps - 1,)),
             dma((mps - 1,)),
-            dma((chunks, seqs - 1)),
-            dma((chunks, seqs - 1)),
+            dma((chunks, 2 * (seqs - 1))),
+            dma((chunks, 2 * (seqs - 1))),
             dma((chunks,)),
             dma((chunks,)),
             dma((chunks,)),
@@ -975,7 +1004,7 @@
             dma((3,)),
         ],
         compiler_params=pltpu.CompilerParams(
-            collective_id=0, has_side_effects=True, vmem_limit_bytes=62 * 1024 * 1024
+            collective_id=0, has_side_effects=True, vmem_limit_bytes=57 * 1024 * 1024
         ),
         name="prefill_pages",
     )(
@@ -995,36 +1024,25 @@
     )
 
 
-def place_kernel(index, offset, text, img, dest, states, out, states_out, rows, state_rows, sems):
+def place_kernel(index, offset, text, img, dest, states, out, states_out, rows, sems):
     parts = index.shape[0]
     block = text.shape[0] // parts
 
-    def load(b):
-        span = pl.ds(b * block, block)
-        return pltpu.make_async_copy(text.at[span, :], rows.at[span, :], sems.at[0, b])
-
     def store(b):
         span = pl.ds(b * block, block)
-        return pltpu.make_async_copy(rows.at[span, :], out.at[span, :], sems.at[1, b])
-
-    state_load = pltpu.make_async_copy(states, state_rows, sems.at[2, 0])
-    state_store = pltpu.make_async_copy(state_rows, states_out, sems.at[2, 1])
-    for b in range(parts):
-        load(b).start()
-    state_load.start()
+        return pltpu.make_async_copy(rows.at[span, :], out.at[span, :], sems.at[b])
+
     for b in range(parts):
         spots = dest[index[b]][:1].astype(jnp.int32) - offset[b]
         hit = lax.broadcasted_iota(jnp.int32, (block, dest.shape[2]), 0) == spots
         placed = jnp.dot(
             jnp.where(hit, 1.0, 0.0).astype(BF16), img[index[b]], preferred_element_type=F32
         )
-        load(b).wait()
         span = pl.ds(b * block, block)
-        rows[span, :] = rows[span, :] + placed.astype(BF16)
+        rows[span, :] = text[span, :] + placed.astype(BF16)
         store(b).start()
-        if b == 0:
-            state_load.wait()
-            state_store.start()
+    state_store = pltpu.make_async_copy(states, states_out, sems.at[parts])
+    state_store.start()
     for b in range(parts):
         store(b).wait()
     state_store.wait()
@@ -1035,21 +1053,22 @@
     smem = pl.BlockSpec(memory_space=pltpu.SMEM)
     vmem = pl.BlockSpec(memory_space=pltpu.VMEM)
     anywhere = pl.BlockSpec(memory_space=pl.ANY)
+    near = [pltpu.with_memory_space_constraint(x, pltpu.VMEM) for x in (text, img, dest, states)]
     return pl.pallas_call(
         place_kernel,
         out_shape=(
             jax.ShapeDtypeStruct(text.shape, text.dtype),
             jax.ShapeDtypeStruct(states.shape, states.dtype),
         ),
-        in_specs=[smem, smem, anywhere, vmem, vmem, anywhere],
+        in_specs=[smem, smem, vmem, vmem, vmem, vmem],
         out_specs=(anywhere, anywhere),
         scratch_shapes=[
             pltpu.VMEM(text.shape, text.dtype),
-            pltpu.VMEM(states.shape, states.dtype),
-            pltpu.SemaphoreType.DMA((3, max(parts, 2))),
+            pltpu.SemaphoreType.DMA((parts + 1,)),
         ],
+        compiler_params=pltpu.CompilerParams(vmem_limit_bytes=16 * 1024 * 1024),
         name="place_images",
-    )(index, offset, text, img, dest, states)
+    )(index, offset, *near)
 
 
 def per_device(

time: 112 us -> 102 us (0.911)
  Pallas kernels: 110 us -> 101 us
    pallas_call x1, Pallas kernels: 103 us -> 97.6 us  [prefill(): pl.pallas_call(functools.partial(prefill_kernel, groups, seqs, mps, promp...]
    pallas_call x1, Pallas kernels: 6.87 us -> 3.08 us  [place(): pl.pallas_call(place_kernel, out_shape=(jax.ShapeDtypeStruct(text.shape,...]
where the time goes in v3:
time: 102 us; the launch traced here: 101 us
  Pallas kernels  101 us (99%)
    pallas_call x1, Pallas kernels, prefill(): pl.pallas_call(functools.partial(prefill_kernel, groups, seqs, mps, promp...  97.6 us
    pallas_call x1, Pallas kernels, place(): pl.pallas_call(place_kernel, out_shape=(jax.ShapeDtypeStruct(text.shape,...  3.08 us

profile of v3, /device:TPU:0, one launch (start us, length us, event | category | flops | bytes accessed | tf_op | source)
XLA Modules:
  0.0 101.3 jit_solution(6441360520021028360)
XLA Ops:
  0.6 97.6 %prefill_pages.1 = (bf16[4096,512]{1,0:T(8,128)(2,1)S(1)}, bf16[128,2048]{1,0:T(8,128)(2,1)S(1)}, bf16[4,128,512]{2,1,0:T(8,128)(2,1)S(1)}, f32[4,8,128]{2,1,0:T(8,128)S(1)}) custom-call(bf16[2048,2048]{1,0:T(8,128)(2,1)} %embeds.1, bf16[128,7296]{1,0:T(8,128)(2,1)} %image_feats.1, bf16[1824,2048]{1,0:T(8,128)(2,1)} %proj_w.1, bf16[2048,2048]{1,0:T(8,128)(2,1)} %kv_w.1, ...), custom_call_target="tpu_custom_call" | custom-call | tf_op jit(solution)/shard_map/prefill_pages/pallas_call | solution.py:902
  98.2 3.1 %place_images.1 = (bf16[4096,512]{1,0:T(8,128)(2,1)}, bf16[128,2048]{1,0:T(8,128)(2,1)}) custom-call(s32[8]{0:T(128)S(1)} %get-tuple-element.14.index, s32[8]{0:T(128)S(1)} %get-tuple-element.15.offset, bf16[4096,512]{1,0:T(8,128)(2,1)S(1)} %get-tuple-element.8.text, bf16[4,128,512]{2,1,0:T(8,128)(2,1)S(1)} %get-tuple-element.9.img, ...), custom_call_target="tpu_custom_call" | custom-call | tf_op jit(solution)/shard_map/place_images/pallas_call | solution.py:1057
  (1 shorter events, 0.0 us)

commit v4 on v3

--- a/solution.py
+++ b/solution.py
@@ -11,6 +11,7 @@
 LANES = 128
 TILE = 256
 CORES = 2
+PIECES = 4
 MESH = pl.DeviceIdType.MESH
 F32 = jnp.float32
 BF16 = jnp.bfloat16
@@ -85,6 +86,8 @@
     p_own,
     p_send,
     p_recv,
+    d_send_buf,
+    d_recv_buf,
     hid,
     i_scaled,
     i_acc,
@@ -123,6 +126,8 @@
     recv_fc,
     send_r,
     recv_r,
+    send_dr,
+    recv_dr,
     send_h,
     recv_h,
     send_i1,
@@ -226,8 +231,6 @@
     for q in range(CORES):
         for k in range(chips):
             w_copy(0, q, k).start()
-    for i in range(1, tiles):
-        e_copy(i).start()
     cache_first = pltpu.make_async_copy(
         kv_cache.at[pl.ds(0, LANES // (queries.shape[1] // HEAD))], cache.at[0], cache_sem.at[0]
     )
@@ -246,6 +249,8 @@
 
 
     f_load.wait()
+    for i in range(1, tiles):
+        e_copy(i).start()
     for b in range(seqs):
         feats[b] = f_rows[:, b * channels : (b + 1) * channels]
     own_feats = pltpu.make_async_copy(feats.at[s], f_buf.at[0], fl_sem)
@@ -361,6 +366,17 @@
             seq=flip(s, 1 << level),
         )
 
+    first_tile = slice(0, col_tile)
+
+    def direct(k):
+        return remote(
+            d_send_buf.at[k - 1],
+            d_recv_buf.at[k - 1],
+            send_dr.at[k - 1],
+            recv_dr.at[k - 1],
+            seq=flip(s, k),
+        )
+
     def scale_tile(i):
         e_copy(i).wait()
 
@@ -386,10 +402,19 @@
         pw_copy.wait()
         spread = f_buf[...].reshape(seqs * half_rows, channels)
 
+        def tile(at):
+            out = jnp.dot(spread, pw_buf[:, at], preferred_element_type=F32)
+            return out.reshape(seqs, half_rows, col_tile)
+
+        out = tile(first_tile)
+        for k in far_first:
+            d_send_buf[k - 1] = out[k].astype(BF16)
+            direct(k).start()
+        p_own[0, :, first_tile] = out[0]
+
         def body(t, carry):
             at = ds(t, col_tile)
-            out = jnp.dot(spread, pw_buf[:, at], preferred_element_type=F32)
-            out = out.reshape(seqs, half_rows, col_tile)
+            out = tile(at)
             for slot_at, e in enumerate(sent_at(0)):
                 p_send[slot_at, :, at] = out[e].astype(BF16)
             p_copy(0, t).start()
@@ -397,7 +422,7 @@
                 p_own[slot_at, :, at] = out[e]
             return carry
 
-        lax.fori_loop(0, col_tiles, body, 0)
+        lax.fori_loop(1, col_tiles, body, 0)
 
     def reduce_level(level):
         def body(t, carry):
@@ -412,7 +437,7 @@
             p_copy(level + 1, t).start()
             return carry
 
-        lax.fori_loop(0, col_tiles, body, 0)
+        lax.fori_loop(1, col_tiles, body, 0)
 
     def combine(p):
         c, i = p // tiles, lax.rem(p, tiles)
@@ -469,20 +494,20 @@
         squares = squares + sq_recv[k - 1]
     scale[...] = mask[...] * lax.rsqrt(squares / width + 1e-05)
 
-    halves = 2
-    piece = block // halves
+    pieces = PIECES
+    piece = block // pieces
 
     def z_piece(c, k, h):
         return remote(
-            by_owner.at[c, ds(flip(s, k) * halves + h, piece), :],
-            arrived.at[c, ds(s * halves + h, piece), :],
-            send_z.at[c, (k - 1) * halves + h],
-            recv_z.at[c, (k - 1) * halves + h],
+            by_owner.at[c, ds(flip(s, k) * pieces + h, piece), :],
+            arrived.at[c, ds(s * pieces + h, piece), :],
+            send_z.at[c, (k - 1) * pieces + h],
+            recv_z.at[c, (k - 1) * pieces + h],
             seq=flip(s, k),
         )
 
     def z_start(c, k):
-        for h in range(halves):
+        for h in range(pieces):
             z_piece(c, k, h).start()
 
     def out_at(rows, half, c):
@@ -553,9 +578,9 @@
         local2(c).start()
 
     def forward(c, k):
-        for h in range(halves):
+        for h in range(pieces):
             z_piece(c, k, h).wait_recv()
-            rows = ds(flip(s, k) * halves + h, piece)
+            rows = ds(flip(s, k) * pieces + h, piece)
 
             @pl.when(g == 0)
             def _():
@@ -632,6 +657,7 @@
     att_copy = pltpu.make_async_copy(attended, states_out, misc_sem.at[1])
 
     batches = rows_dec // batch
+    early = batches * 5 // 16
 
     def attend_start():
         for j in range(heads):
@@ -669,20 +695,28 @@
         finish(c)
         z_start(c, 1)
         own_sends(c)
+    attend(0, early)
     forward(0, 1)
     forward(0, seqs - 1)
 
     own_rows = ds(g, half_rows)
+
+    def activate(total, t, at):
+        total = total + bias_rows[pl.ds(t, 1), :]
+        hid[own_rows, at] = (0.5 * total * (1.0 + lax.erf(total * 0.5**0.5))).astype(BF16)
 
     def gelu_body(t, carry):
         at = ds(t, col_tile)
         p_copy(levels - 1, t).wait()
-        total = p_own[0, :, at] + p_recv[base_at(levels - 1), :, at].astype(F32)
-        total = total + bias_rows[pl.ds(t, 1), :]
-        hid[own_rows, at] = (0.5 * total * (1.0 + lax.erf(total * 0.5**0.5))).astype(BF16)
+        activate(p_own[0, :, at] + p_recv[base_at(levels - 1), :, at].astype(F32), t, at)
         return carry
 
-    lax.fori_loop(0, col_tiles, gelu_body, 0)
+    total = p_own[0, :, first_tile]
+    for k in range(1, seqs):
+        direct(k).wait()
+        total = total + d_recv_buf[k - 1].astype(F32)
+    activate(total, 0, first_tile)
+    lax.fori_loop(1, col_tiles, gelu_body, 0)
     h_send = remote(hid.at[own_rows, :], hid.at[own_rows, :], send_h, recv_h, group=peer)
 
     @pl.when(g != 0)
@@ -735,6 +769,12 @@
             is2[k - 1, b] = total[:, k * LANES : (k + 1) * LANES].astype(BF16)
     for k in range(1, chips):
         i_second(k).start()
+
+    @pl.when(g == 0)
+    def _():
+        for c in range(chunks):
+            take_peer(c)
+
     for k in range(1, mps):
         iq_send(k).wait()
     squares = isq_own[...]
@@ -763,7 +803,7 @@
     i_local.start()
     for c in range(1, chunks):
         z_start(c, seqs // 2)
-    attend(0, batches)
+    attend(early, batches)
     for k in far_first:
         if k not in (1, seqs - 1):
             forward(0, k)
@@ -775,11 +815,6 @@
         )
 
 
-    @pl.when(g == 0)
-    def _():
-        for c in range(chunks):
-            take_peer(c)
-
     hid_copy = pltpu.make_async_copy(hid, states_out, misc_sem.at[1])
 
     @pl.when(g == 0)
@@ -788,15 +823,17 @@
         hid_copy.start()
 
     rest = [k for k in far_first if k != 1]
-    for c in range(1, chunks):
-
-        @pl.when(outer)
-        def _():
+
+    @pl.when(outer)
+    def _():
+        for c in range(1, chunks):
             forward(c, rest[0])
 
-        @pl.when(jnp.logical_not(outer))
-        def _():
-            forward(c, rest[-1])
+    @pl.when(jnp.logical_not(outer))
+    def _():
+        for c in range(1, chunks):
+            for k in reversed(rest):
+                forward(c, k)
 
     for k in far_first:
         iz_send(k).wait_recv()
@@ -805,22 +842,15 @@
         def _():
             if_send(k).start()
 
-    for c in range(1, chunks):
-
-        @pl.when(outer)
-        def _():
+    @pl.when(outer)
+    def _():
+        for c in range(1, chunks):
             for k in rest[1:]:
                 forward(c, k)
 
-        @pl.when(jnp.logical_not(outer))
-        def _():
-            for k in rest[:-1]:
-                forward(c, k)
-
-
     for c in range(chunks):
         for k in range(1, seqs):
-            for h in range(halves):
+            for h in range(pieces):
                 z_piece(c, k, h).wait_send()
         local(by_owner.at[c], everything, c).wait()
 
@@ -939,6 +969,8 @@
             pltpu.VMEM((seqs // 2, half_rows, feat_local), F32),
             pltpu.VMEM((seqs - 1, half_rows, feat_local), BF16),
             pltpu.VMEM((seqs - 1, half_rows, feat_local), BF16),
+            pltpu.VMEM((seqs - 1, half_rows, col_tile), BF16),
+            pltpu.VMEM((seqs - 1, half_rows, col_tile), BF16),
             pltpu.VMEM((rows_img, feat_local), BF16),
             pltpu.VMEM((half_rows, feat_local), BF16),
             pltpu.VMEM((blocks, half_rows, chips * LANES), F32),
@@ -977,6 +1009,8 @@
             dma((seqs - 1,)),
             dma((levels, col_tiles)),
             dma((levels, col_tiles)),
+            dma((seqs - 1,)),
+            dma((seqs - 1,)),
             dma,
             dma,
             dma,
@@ -985,8 +1019,8 @@
             dma((chips - 1,)),
             dma((mps - 1,)),
             dma((mps - 1,)),
-            dma((chunks, 2 * (seqs - 1))),
-            dma((chunks, 2 * (seqs - 1))),
+            dma((chunks, PIECES * (seqs - 1))),
+            dma((chunks, PIECES * (seqs - 1))),
             dma((chunks,)),
             dma((chunks,)),
             dma((chunks,)),

time: 102 us -> 98.1 us (0.962)
  Pallas kernels: 101 us -> 96.8 us
    pallas_call x1, Pallas kernels: 97.6 us -> 93.7 us  [prefill(): pl.pallas_call(functools.partial(prefill_kernel, groups, seqs, mps, promp...]
where the time goes in v4:
time: 98.1 us; the launch traced here: 97.5 us
  Pallas kernels  96.8 us (99%)
    pallas_call x1, Pallas kernels, prefill(): pl.pallas_call(functools.partial(prefill_kernel, groups, seqs, mps, promp...  93.7 us
    pallas_call x1, Pallas kernels, place(): pl.pallas_call(place_kernel, out_shape=(jax.ShapeDtypeStruct(text.shape,...  3.08 us

profile of v4, /device:TPU:0, one launch (start us, length us, event | category | flops | bytes accessed | tf_op | source)
XLA Modules:
  0.0 97.5 jit_solution(17851309801044795016)
XLA Ops:
  0.6 93.7 %prefill_pages.1 = (bf16[4096,512]{1,0:T(8,128)(2,1)S(1)}, bf16[128,2048]{1,0:T(8,128)(2,1)S(1)}, bf16[4,128,512]{2,1,0:T(8,128)(2,1)S(1)}, f32[4,8,128]{2,1,0:T(8,128)S(1)}) custom-call(bf16[2048,2048]{1,0:T(8,128)(2,1)} %embeds.1, bf16[128,7296]{1,0:T(8,128)(2,1)} %image_feats.1, bf16[1824,2048]{1,0:T(8,128)(2,1)} %proj_w.1, bf16[2048,2048]{1,0:T(8,128)(2,1)} %kv_w.1, ...), custom_call_target="tpu_custom_call" | custom-call | tf_op jit(solution)/shard_map/prefill_pages/pallas_call | solution.py:932
  94.4 3.1 %place_images.1 = (bf16[4096,512]{1,0:T(8,128)(2,1)}, bf16[128,2048]{1,0:T(8,128)(2,1)}) custom-call(s32[8]{0:T(128)S(1)} %get-tuple-element.14.index, s32[8]{0:T(128)S(1)} %get-tuple-element.15.offset, bf16[4096,512]{1,0:T(8,128)(2,1)S(1)} %get-tuple-element.8.text, bf16[4,128,512]{2,1,0:T(8,128)(2,1)S(1)} %get-tuple-element.9.img, ...), custom_call_target="tpu_custom_call" | custom-call | tf_op jit(solution)/shard_map/place_images/pallas_call | solution.py:1091
  (1 shorter events, 0.0 us)

commit v5 on v4

--- a/solution.py
+++ b/solution.py
@@ -387,7 +387,7 @@
                 at = slice(j * LANES, (j + 1) * LANES)
                 value = e_buf[rows, at].astype(F32)
                 total = total + value * value
-                e_buf[rows, at] = (value * gain_rows[j : j + 1, :]).astype(BF16)
+                e_buf[rows, at] = e_buf[rows, at] * gain_rows[j : j + 1, :].astype(BF16)
             sq_own[pl.ds(i * (TILE // LANES) + b, 1), :] = jnp.sum(
                 jnp.transpose(total), axis=0, keepdims=True
             )

time: 98.1 us -> 98.1 us (level)
  no operation moved by 1% of the time
where the time goes in v5:
time: 98.1 us; the launch traced here: 97.4 us
  Pallas kernels  96.8 us (99%)
    pallas_call x1, Pallas kernels, prefill(): pl.pallas_call(functools.partial(prefill_kernel, groups, seqs, mps, promp...  93.7 us
    pallas_call x1, Pallas kernels, place(): pl.pallas_call(place_kernel, out_shape=(jax.ShapeDtypeStruct(text.shape,...  3.08 us

profile of v5, /device:TPU:0, one launch (start us, length us, event | category | flops | bytes accessed | tf_op | source)
XLA Modules:
  0.0 97.4 jit_solution(345615991843071768)
XLA Ops:
  0.6 93.7 %prefill_pages.1 = (bf16[4096,512]{1,0:T(8,128)(2,1)S(1)}, bf16[128,2048]{1,0:T(8,128)(2,1)S(1)}, bf16[4,128,512]{2,1,0:T(8,128)(2,1)S(1)}, f32[4,8,128]{2,1,0:T(8,128)S(1)}) custom-call(bf16[2048,2048]{1,0:T(8,128)(2,1)} %embeds.1, bf16[128,7296]{1,0:T(8,128)(2,1)} %image_feats.1, bf16[1824,2048]{1,0:T(8,128)(2,1)} %proj_w.1, bf16[2048,2048]{1,0:T(8,128)(2,1)} %kv_w.1, ...), custom_call_target="tpu_custom_call" | custom-call | tf_op jit(solution)/shard_map/prefill_pages/pallas_call | solution.py:932
  94.4 3.1 %place_images.1 = (bf16[4096,512]{1,0:T(8,128)(2,1)}, bf16[128,2048]{1,0:T(8,128)(2,1)}) custom-call(s32[8]{0:T(128)S(1)} %get-tuple-element.14.index, s32[8]{0:T(128)S(1)} %get-tuple-element.15.offset, bf16[4096,512]{1,0:T(8,128)(2,1)S(1)} %get-tuple-element.8.text, bf16[4,128,512]{2,1,0:T(8,128)(2,1)S(1)} %get-tuple-element.9.img, ...), custom_call_target="tpu_custom_call" | custom-call | tf_op jit(solution)/shard_map/place_images/pallas_call | solution.py:1091
  (1 shorter events, 0.0 us)
